TPU v7x, 512 devices: a whole 4x4x16 slice. The times are simulated.
512 devices in a mesh: dp: 32 (over y, x, core), mp: 16 (over z).
Axes of the slice: x: 4, y: 4, z: 16, core: 2. Of those that a mesh axis runs over, the one named last changes fastest.
Arguments:
- task_codes: bfloat16 [64, 128], replicated, may hold values from -6 to 6
- hyper_weight: bfloat16 [128, 196608], P(None, ('dp', 'mp')), may hold values from -0.5 to 0.5
- frozen_weight: bfloat16 [5120, 1024], P('mp'), may hold values from -0.125 to 0.125
- tokens: bfloat16 [131072, 5120], P(('dp', 'mp')), may hold values from -6 to 6
- teacher: bfloat16 [131072, 1024], P(('dp', 'mp')), may hold values from -6 to 6
- seq_slot: int32 [1024], P(('dp', 'mp')), may hold values from 0 to 3, as said below
- task_share: int32 [32], replicated, may hold values from 1 to 4, as said below
- token_counts: int32 [64], replicated, may hold values from 1024 to 3071
Outputs:
- hyper_grad: float32 [128, 196608], P(None, ('dp', 'mp'))
Inputs may be any that keep to these rules, and one draw needn't show every extreme that they name: Group g owns task_share[g] tasks, numbered after those of groups 0 to g - 1; the entries sum to 64; in every draw some group owns exactly 4 tasks. For sequence s of group g = s // 32, seq_slot[s] < task_share[g]; in every group some sequence names the group's last task.
All inputs are finite; a program needn't handle non-finite values.
Results may differ from a plain program's by a relative error of at most 0.012.
Values may be sent and summed in bfloat16 or wider, within the bound.
A program may use at most 64 MiB of HBM per device.

v0:
```python
import math

import jax
import jax.numpy as jnp
from jax import lax
from jax.sharding import PartitionSpec as P

D = 5120
KV = 1024
R = 32
TPG = 4
SEQ_LEN = 128


def shards(
    task_codes, hyper_weight, frozen_weight, tokens, teacher, seq_slot, task_share, token_counts
):
    groups = lax.axis_size("dp")
    members = lax.axis_size("mp")
    tok_dev = tokens.shape[0]
    shard_cols = hyper_weight.shape[1]
    shrink_factor = 1.0 / math.sqrt(D)
    rank_scale = 1.0 / math.sqrt(R)
    loss_scale = 1.0 / math.sqrt(tok_dev * members)
    slot_iota = jnp.arange(TPG, dtype=jnp.int32)
    offsets = jnp.cumsum(task_share) - task_share
    slot_live = slot_iota[:, None] < task_share[None, :]
    slot_task = jnp.where(slot_live, offsets[None, :] + slot_iota[:, None], 0).reshape(-1)
    live_rows = slot_live.reshape(-1, 1)
    adapters = jnp.dot(task_codes, hyper_weight, preferred_element_type=jnp.float32).astype(
        jnp.bfloat16
    )
    picked = jnp.where(
        live_rows, jnp.take(adapters, slot_task, axis=0), jnp.zeros((), jnp.bfloat16)
    )
    blocks = lax.all_to_all(
        picked.reshape(TPG, groups, 1, shard_cols), "dp", split_axis=1, concat_axis=1, tiled=True
    )
    own_adapters = lax.all_gather(blocks, "mp", axis=2, tiled=True).reshape(TPG, -1)
    adapter_input = own_adapters[:, : D * R].reshape(TPG, D, R)
    adapter_out = own_adapters[:, D * R :].reshape(TPG * R, KV)
    tok_slot = jnp.repeat(seq_slot, SEQ_LEN)
    onehot = (tok_slot[:, None] == slot_iota[None, :]).astype(jnp.float32)
    frozen_out = jnp.dot(
        tokens,
        lax.all_gather(frozen_weight, "mp", axis=0, tiled=True),
        preferred_element_type=jnp.float32,
    )
    low_all = jnp.einsum("td,sdr->tsr", tokens, adapter_input, preferred_element_type=jnp.float32)
    compact_factor_carry = (
        (low_all * (onehot[:, :, None] * shrink_factor))
        .astype(jnp.bfloat16)
        .reshape(tok_dev, TPG * R)
    )
    adapter_term = (
        jnp.dot(compact_factor_carry, adapter_out, preferred_element_type=jnp.float32) * rank_scale
    )
    counts = token_counts.astype(jnp.float32)
    task_weight = jnp.mean(counts) / counts
    own_offset = jnp.take(offsets, lax.axis_index("dp"))
    slot_weight = jnp.take(task_weight, jnp.minimum(own_offset + slot_iota, counts.shape[0] - 1))
    token_weight = jnp.sum(onehot * slot_weight[None, :], axis=1) * loss_scale
    value_grad = (
        (frozen_out + adapter_term - teacher.astype(jnp.float32)) * token_weight[:, None]
    ).astype(jnp.bfloat16)
    low_grad_all = (
        jnp.einsum("tk,ck->tc", value_grad, adapter_out, preferred_element_type=jnp.float32)
        * rank_scale
    )
    narrow_derivative = (low_grad_all.reshape(tok_dev, TPG, R) * onehot[:, :, None]).astype(
        jnp.bfloat16
    )
    primary_derivative = (
        jnp.einsum("td,tsr->sdr", tokens, narrow_derivative, preferred_element_type=jnp.float32)
        * shrink_factor
    )
    second_grad = (
        jnp.einsum(
            "tc,tk->ck", compact_factor_carry, value_grad, preferred_element_type=jnp.float32
        )
        * rank_scale
    )
    device_grad = jnp.concatenate(
        [primary_derivative.reshape(TPG, D * R), second_grad.reshape(TPG, R * KV)], axis=1
    )
    rounded = lax.optimization_barrier(device_grad.astype(jnp.bfloat16)).reshape(
        TPG, groups, members, shard_cols
    )
    routed = lax.all_to_all(rounded, "dp", split_axis=1, concat_axis=1, tiled=True)
    summed = lax.psum_scatter(
        routed.astype(jnp.float32).astype(jnp.bfloat16), "mp", scatter_dimension=2, tiled=True
    ).astype(jnp.float32)
    task_iota = jnp.arange(counts.shape[0], dtype=jnp.int32)
    select = ((slot_task[None, :] == task_iota[:, None]) & slot_live.reshape(1, -1)).astype(
        jnp.float32
    )
    adapter_grad = jnp.dot(select, summed.reshape(-1, shard_cols), precision=lax.Precision.HIGHEST)
    return jnp.dot(task_codes.astype(jnp.float32).T, adapter_grad, precision=lax.Precision.HIGHEST)


def solution(mesh):
    placed = (
        P(),
        P(None, ("dp", "mp")),
        P("mp", None),
        P(("dp", "mp"), None),
        P(("dp", "mp"), None),
        P(("dp", "mp")),
        P(),
        P(),
    )
    return jax.shard_map(
        shards, mesh=mesh, in_specs=placed, out_specs=P(None, ("dp", "mp")), check_vma=False
    )
```

profile of v0, /device:TPU:2, one launch (start us, length us, event | category | flops | bytes accessed | tf_op | source)
XLA Modules:
  0.0 364.2 jit_solution(9389293065033132992)
XLA Ops:
  6.5 0.9 copy.17
  9.9 1.1 convolution_convert_fusion
  11.0 0.9 gather_fusion
  12.0 15.0 %all_to_all.10 = bf16[4,32,1,384]{3,0,2,1:T(4,128)(2,1)S(1)} all-to-all(bf16[4,32,1,384]{3,0,2,1:T(4,128)(2,1)S(1)} %fusion.19), channel_id=1, replica_groups=mesh['dp'=32,'mp'=16] {'dp'}, dimensions={1} | all-to-all | bytes 196608 | tf_op jit(solution)/shard_map/all_to_all | solution.py:36
  29.1 1.3 convert_reduce_fusion
  33.0 67.2 %all-gather.5.cloned.1.call-done = bf16[4,32,16,384]{3,1,0,2:T(8,128)(2,1)} async-done(((bf16[4,32,1,384]{3,1,0,2:T(8,128)(2,1)}), bf16[4,32,16,384]{3,1,0,2:T(8,128)(2,1)}) %all-gather.5.cloned.1.call-update) | async-done | bytes 1572880 | tf_op jit(solution)/shard_map/all_gather | solution.py:39
  100.2 2.3 copy.22
  102.5 1.2 copy.29
  103.9 1.5 slice.17
  105.6 3.7 %reshape.348 = bf16[655360]{0:T(1024)(128)(2,1)} reshape(bf16[4,163840]{1,0:T(4,128)(2,1)} %slice.17) | data formatting | bytes 2621440
  109.3 6.6 %reshape.293 = bf16[4,5120,32]{2,1,0:T(8,128)(2,1)} reshape(bf16[655360]{0:T(1024)(128)(2,1)} %reshape.348) | data formatting | bytes 2621440 | tf_op jit(solution)/shard_map/reshape | solution.py:40
  115.9 4.0 %fusion.16 = bf16[256,4,32]{0,2,1:T(8,128)(2,1)S(1)} fusion(bf16[4,5120,32]{2,1,0:T(8,128)(2,1)} %reshape.293, bf16[256,5120]{1,0:T(8,128)(2,1)S(1)} %copy-done, f32[256,4]{0,1:T(4,128)S(1)} %get-tuple-element.17), kind=kOutput, calls=%fused_computation.20 | convolution fusion | flops 335609856 | bytes 4001792 | tf_op jit(solution)/shard_map/td,sdr->tsr/dot_general | solution.py:49
  120.0 106.4 %all-gather.3.cloned.1.call-done = bf16[5120,1024]{1,0:T(8,128)(2,1)} async-done(((bf16[320,1024]{1,0:T(8,128)(2,1)}), bf16[5120,1024]{1,0:T(8,128)(2,1)}) %all-gather.3.cloned.1.call-update) | async-done | bytes 10485776 | tf_op jit(solution)/shard_map/all_gather | solution.py:46
  226.3 5.6 %fusion.30 = f32[256,1024]{1,0:T(8,128)S(1)} fusion(bf16[256,5120]{1,0:T(8,128)(2,1)S(1)} %copy-done, bf16[5120,1024]{1,0:T(8,128)(2,1)} %all-gather.3.cloned.1.call-done), kind=kOutput, calls=%fused_computation.53 | convolution fusion | flops 2684354560 | bytes 14155776 | tf_op jit(solution)/shard_map/dot_general | solution.py:44
  233.1 1.7 fusion.1
  234.8 5.3 %copy.24 = bf16[4,5120,32]{2,1,0:T(8,128)(2,1)} copy(bf16[4,5120,32]{1,2,0:T(8,128)(2,1)} %fusion.1) | data formatting | bytes 2621440 | tf_op jit(solution)/shard_map/mul | solution.py:74
  240.0 7.1 %reshape.350 = bf16[655360]{0:T(1024)(128)(2,1)} reshape(bf16[4,5120,32]{2,1,0:T(8,128)(2,1)} %copy.24) | data formatting | bytes 2621440
  247.2 2.9 reshape.297
  250.1 6.2 %pad_maximum_fusion = bf16[4,196608]{1,0:T(4,128)(2,1)S(1)} fusion(bf16[4,32768]{1,0:T(4,128)(2,1)S(1)} %reshape.298, bf16[4,163840]{1,0:T(4,128)(2,1)} %reshape.297), kind=kLoop, calls=%fused_computation.8 | loop fusion | flops 3145728 | bytes 3145728 | tf_op jit(solution)/shard_map/concatenate | solution.py:83
  256.2 28.8 %all_to_all.11 = bf16[4,32,16,384]{3,0,2,1:T(4,128)(2,1)S(1)} all-to-all(bf16[4,32,16,384]{3,0,2,1:T(4,128)(2,1)S(1)} %bitcast.54), channel_id=1, replica_groups=mesh['dp'=32,'mp'=16] {'dp'}, dimensions={1} | all-to-all | bytes 3145728 | tf_op jit(solution)/shard_map/all_to_all | solution.py:89
  285.1 2.1 copy.26
  287.3 68.1 %reduce-scatter.2.cloned.1.call-done = bf16[4,32,1,384]{3,1,0,2:T(8,128)(2,1)} async-done(((bf16[4,32,16,384]{3,1,0,2:T(8,128)(2,1)}), bf16[4,32,1,384]{3,1,0,2:T(8,128)(2,1)}) %reduce-scatter.2.cloned.1.call-update) | async-done | bytes 98320 | tf_op jit(solution)/shard_map/reduce_scatter | solution.py:90
  355.5 1.0 fusion.22
  356.9 0.8 copy.27
  (46 shorter events, 8.1 us)
Async XLA Ops:
  6.5 109.4 %copy-start = (bf16[256,5120]{1,0:T(8,128)(2,1)S(1)}, bf16[256,5120]{1,0:T(8,128)(2,1)}, u32[]{:S(2)}) copy-start(bf16[256,5120]{1,0:T(8,128)(2,1)} %param.11) | copy-start | bytes 7864324
  6.5 26.3 %copy-start.3 = (s32[2]{0:T(128)S(1)}, s32[2]{0:T(128)}, u32[]{:S(2)}) copy-start(s32[2]{0:T(128)} %param.13) | copy-start | bytes 28
  6.5 93.7 %all-gather.5.cloned.1.call-start = ((), (), s32[]{:S(2)}) async-start(), calls=%async_computation.4 | async-start | bytes 1671168 | tf_op jit(solution)/shard_map/all_gather | solution.py:39
  27.6 198.7 %all-gather.3.cloned.1.call-start = ((), (), s32[]{:S(2)}) async-start(), calls=%async_computation.3 | async-start | bytes 11141120 | tf_op jit(solution)/shard_map/all_gather | solution.py:46
  28.4 327.1 %reduce-scatter.2.cloned.1.call-start = ((), (), s32[]{:S(2)}) async-start(), calls=%async_computation.5 | async-start | bytes 1671168 | tf_op jit(solution)/shard_map/reduce_scatter | solution.py:90
  226.3 5.6 %copy-start.1 = (bf16[256,1024]{1,0:T(8,128)(2,1)S(1)}, bf16[256,1024]{1,0:T(8,128)(2,1)}, u32[]{:S(2)}) copy-start(bf16[256,1024]{1,0:T(8,128)(2,1)} %param.12) | copy-start | bytes 1572868
  285.1 71.4 %copy-start.2 = (bf16[64,128]{1,0:T(8,128)(2,1)S(1)}, bf16[64,128]{1,0:T(8,128)(2,1)}, u32[]{:S(2)}) copy-start(bf16[64,128]{1,0:T(8,128)(2,1)} %param.8) | copy-start | bytes 49156
Sparse Core Ops, SparseCore 0:
  27.8 72.3 all-gather.4
  102.3 123.9 all-gather.2
  287.3 68.1 reduce-scatter.1
where the time goes:
time: 365 us; the launch traced here: 364 us
  waiting for transfers between devices  242 us (66%)
  blocking collectives  43.8 us (12%)
  local copies, waits for them, and re-layouts  38.2 us (10%)
  matrix products  14.7 us (4%)
  between operations  14.4 us (4%)
  other arithmetic  10.5 us (3%)
    all_gather x1, waiting for transfers between devices, shards(): lax.all_gather(frozen_weight, 'mp', axis=0, tiled=True)  106 us
    reduce_scatter x1, waiting for transfers between devices, shards(): lax.psum_scatter(routed.astype(jnp.float32).astype(jnp.bfloat16), 'mp', s...  68.1 us
    all_gather x1, waiting for transfers between devices, shards(): lax.all_gather(blocks, 'mp', axis=2, tiled=True).reshape(TPG, -1)  67.2 us
    all_to_all x1, blocking collectives, shards(): lax.all_to_all(rounded, 'dp', split_axis=1, concat_axis=1, tiled=True)  28.8 us
    all_to_all x1, blocking collectives, shards(): lax.all_to_all(picked.reshape(TPG, groups, 1, shard_cols), 'dp', split_ax...  15 us
    unnamed x11, local copies, waits for them, and re-layouts  12.1 us
  transfers between devices with their start and end apart: 3, of which 3 were waited for; matrix products, arithmetic and copies ran while one was open for 6% of the time, Pallas kernels for 0%

commit v1 on v0

v1 whole, which is shorter than its diff:
```python
import math

import jax
import jax.numpy as jnp
from jax import lax
from jax.experimental import pallas as pl
from jax.experimental.pallas import tpu as pltpu
from jax.sharding import PartitionSpec as P

D = 5120
KV = 1024
R = 32
TPG = 4
SEQ_LEN = 128
GROUPS = 32
MEMBERS = 16
SIDE = 4
TASKS = 64
TOK = 256
BLK = D // MEMBERS
SLICE = BLK // SIDE
ROWS = 3 * TPG * GROUPS
PIECES = 2
PIECE = ROWS // PIECES
HALF = MEMBERS // 2
TALL = 192 * GROUPS
MESH = pl.DeviceIdType.MESH
F32 = jnp.float32
BF16 = jnp.bfloat16
LOSS_SCALE = 1.0 / math.sqrt(TOK * MEMBERS)
SHRINK = 1.0 / math.sqrt(D)
RANK_SCALE = 1.0 / math.sqrt(R)


def dot(a, b):
    return jnp.dot(a, b, preferred_element_type=F32)


def iota(shape, axis):
    return lax.broadcasted_iota(jnp.int32, shape, axis)


def step_kernel(
    codes_ref,
    hyper_ref,
    frozen_hbm,
    tokens_hbm,
    teacher_hbm,
    seq_ref,
    share_ref,
    counts_ref,
    out_ref,
    w_buf,
    tok_buf,
    teach_buf,
    perm_buf,
    stage,
    send_small,
    recv_small,
    send_back,
    recv_back,
    ag_buf,
    tall,
    low_rows,
    b_mat,
    acc,
    own,
    send_run,
    recv_run,
    local_sem,
    small_s,
    small_r,
    back_s,
    back_r,
    wz_s,
    wz_r,
    p1_s,
    p1_r,
    p2_s,
    p2_r,
    die_s,
    die_r,
    ag_s,
    ag_r,
    rs_s,
    rs_r,
):
    dp = lax.axis_index("dp")
    z = lax.axis_index("mp")
    c = lax.rem(dp, 2)
    x = lax.rem(dp // 2, SIDE)
    y = dp // (2 * SIDE)
    f = 1 - 2 * c

    def wrap(value, size):
        return lax.rem(value + 2 * size, size)

    def place(yy, xx):
        return (yy * SIDE + xx) * 2 + c

    def remote(src, dst, ssem, rsem, to_dp, to_z):
        return pltpu.make_async_remote_copy(
            src_ref=src,
            dst_ref=dst,
            send_sem=ssem,
            recv_sem=rsem,
            device_id=(to_dp, to_z),
            device_id_type=MESH,
        )

    sent = []

    def send(src, dst, ssem, rsem, to_dp, to_z):
        copy = remote(src, dst, ssem, rsem, to_dp, to_z)
        copy.start()
        sent.append(copy)

    def arrive(dst, ssem, rsem):
        remote(dst, dst, ssem, rsem, dp, z).wait_recv()

    barrier = pltpu.get_barrier_semaphore()

    @pl.loop(1, GROUPS)
    def _(i):
        pl.semaphore_signal(
            barrier, inc=1, device_id=(lax.rem(dp + i, GROUPS), z), device_id_type=MESH
        )

    for shift in (1, -1):
        pl.semaphore_signal(
            barrier, inc=1, device_id=(dp, wrap(z + shift, MEMBERS)), device_id_type=MESH
        )

    local = []
    for yy in range(SIDE):
        for cc in range(2):
            local.append(
                pltpu.make_async_copy(
                    frozen_hbm.at[:, pl.ds((2 * yy + cc) * 128, 128)],
                    w_buf.at[yy, cc, pl.ds(pl.multiple_of(BLK * z, 16), BLK), :],
                    local_sem.at[2 * yy + cc],
                )
            )
    tok_copy = pltpu.make_async_copy(tokens_hbm, tok_buf, local_sem.at[8])
    teach_copy = pltpu.make_async_copy(teacher_hbm, teach_buf, local_sem.at[9])
    for copy in local:
        copy.start()
    tok_copy.start()
    teach_copy.start()

    share = share_ref[...].astype(F32)
    g_row = lax.rem(iota((TPG * GROUPS, GROUPS), 0), GROUPS)
    g_col = iota((TPG * GROUPS, GROUPS), 1)
    share_all = jnp.broadcast_to(share, (TPG * GROUPS, GROUPS))
    first = jnp.sum(jnp.where(g_col < g_row, share_all, 0.0), axis=1, keepdims=True)
    mine = jnp.sum(jnp.where(g_col == g_row, share_all, 0.0), axis=1, keepdims=True)
    slot_row = (iota((TPG * GROUPS, TASKS), 0) // GROUPS).astype(F32)
    task_col = iota((TPG * GROUPS, TASKS), 1).astype(F32)
    picks = (task_col == first + slot_row) & (slot_row < mine)
    codes_sel = dot(jnp.where(picks, 1.0, 0.0).astype(BF16), codes_ref[...]).astype(BF16)
    stage[pl.ds(ROWS, 128), :] = jnp.zeros((128, 128), F32)
    for s in range(3):
        cols = dot(codes_sel, hyper_ref[:, 128 * s : 128 * (s + 1)]).astype(BF16).astype(F32)
        for slot in range(TPG):
            stage[pl.ds((slot * 3 + s) * GROUPS, GROUPS), :] = cols[
                slot * GROUPS : (slot + 1) * GROUPS
            ]

    @pl.loop(0, GROUPS)
    def _(g):
        send_small[g] = stage[pl.ds(g, 16, stride=GROUPS), :].astype(BF16)

    row = iota((512, 512), 0)
    target = lax.rem(row // 32, 4) * 128 + (row // 128) * 32 + lax.rem(row, 32)
    perm_buf[...] = jnp.where(iota((512, 512), 1) == target, 1.0, 0.0).astype(BF16)

    pl.semaphore_wait(barrier, GROUPS + 1)

    @pl.loop(1, GROUPS)
    def _(i):
        to = lax.rem(dp + i, GROUPS)
        remote(
            send_small.at[to], recv_small.at[dp], small_s.at[i], small_r.at[i], to, z
        ).start()

    for copy in local:
        copy.wait()

    def w_block(way, d):
        return wrap(z - f * d if way == 0 else z + f * d, MEMBERS)

    def w_rows(start, size):
        return pl.ds(pl.multiple_of(start, 16), size)

    def w_slice(zb):
        return w_buf.at[y, c, w_rows(BLK * zb + SLICE * x, SLICE), :]

    def w_piece(way, phase, zb, i):
        if way == 0 and phase == 1:
            return w_buf.at[y, c, w_rows(BLK * zb + SLICE * i, SLICE), :]
        if way == 0:
            return w_buf.at[i, c, w_rows(BLK * zb, BLK), :]
        if phase == 1:
            return w_buf.at[i, c, w_rows(BLK * zb + SLICE * x, SLICE), :]
        return w_buf.at[:, c, w_rows(BLK * zb + SLICE * i, SLICE), :]

    def along(way, phase):
        return x if (way == 0) == (phase == 1) else y

    def shifted(way, phase, by):
        if (way == 0) == (phase == 1):
            return place(y, wrap(x + by, SIDE))
        return place(wrap(y + by, SIDE), x)

    def w_reach(way):
        return HALF if way == 0 else HALF - 1

    def z_to(way):
        return wrap(z + f if way == 0 else z - f, MEMBERS)

    def send_z(way, d):
        ref = w_slice(w_block(way, d - 1))
        send(ref, ref, wz_s.at[way, d - 1], wz_r.at[way, d - 1], dp, z_to(way))

    def start_phase(way, phase, d):
        sems, semr = (p1_s, p1_r) if phase == 1 else (p2_s, p2_r)
        ref = w_piece(way, phase, w_block(way, d), along(way, phase))
        send(ref, ref, sems.at[way, d - 1, 0], semr.at[way, d - 1, 0], shifted(way, phase, f), z)
        send(ref, ref, sems.at[way, d - 1, 1], semr.at[way, d - 1, 1], shifted(way, phase, -f), z)

    def pass_on(way, phase, d):
        sems, semr = (p1_s, p1_r) if phase == 1 else (p2_s, p2_r)
        ref = w_piece(way, phase, w_block(way, d), wrap(along(way, phase) - f, SIDE))
        arrive(ref, sems.at[way, d - 1, 0], semr.at[way, d - 1, 0])
        send(ref, ref, sems.at[way, d - 1, 2], semr.at[way, d - 1, 2], shifted(way, phase, f), z)

    def end_phase(way, phase, d):
        sems, semr = (p1_s, p1_r) if phase == 1 else (p2_s, p2_r)
        zb = w_block(way, d)
        at = along(way, phase)
        arrive(
            w_piece(way, phase, zb, wrap(at + f, SIDE)),
            sems.at[way, d - 1, 1],
            semr.at[way, d - 1, 1],
        )
        arrive(
            w_piece(way, phase, zb, wrap(at - 2 * f, SIDE)),
            sems.at[way, d - 1, 2],
            semr.at[way, d - 1, 2],
        )

    def die_part(way, d, core):
        return w_buf.at[:, core, w_rows(BLK * w_block(way, d), BLK), :]

    def start_die(way, d):
        ref = die_part(way, d, c)
        send(ref, ref, die_s.at[way, d - 1], die_r.at[way, d - 1], dp + f, z)

    def end_die(way, d):
        other = wrap(z + f * d if way == 0 else z - f * d, MEMBERS)
        ref = w_buf.at[:, 1 - c, w_rows(BLK * other, BLK), :]
        arrive(ref, die_s.at[way, d - 1], die_r.at[way, d - 1])

    def ag_piece(way, d, p):
        return ag_buf.at[w_block(way, d), pl.ds(p * PIECE, PIECE), :]

    def send_ag(way, d, p):
        ref = ag_piece(way, d - 1, p)
        send(ref, ref, ag_s.at[way, d - 1, p], ag_r.at[way, d - 1, p], dp, z_to(way))

    def get_ag(way, d):
        for p in range(PIECES):
            arrive(ag_piece(way, d, p), ag_s.at[way, d - 1, p], ag_r.at[way, d - 1, p])
            if d < w_reach(way):
                send_ag(way, d + 1, p)

    def spread(m):
        block = jnp.concatenate(
            [ag_buf[m, pl.ds(96 * slot, 96), :] for slot in range(TPG)], axis=1
        )
        moved = dot(block, perm_buf[...])
        for s in range(3):
            for j in range(4):
                tall[pl.ds(12 * m + 4 * s + j, GROUPS, stride=192), :] = moved[
                    32 * s : 32 * (s + 1), 128 * j : 128 * (j + 1)
                ]
        for slot in range(TPG):
            for s in range(3):
                last = ag_buf[m, pl.ds(96 * slot + 32 * s + 16, 16), :].astype(F32)
                low_rows[slot, pl.ds(3 * m + s, 8, stride=48), :] = last[8:16]

    for way in (0, 1):
        send_z(way, 1)

    recv_small[dp] = send_small[dp]

    @pl.loop(1, GROUPS)
    def _(i):
        frm = wrap(dp - i, GROUPS)
        arrive(recv_small.at[frm], small_s.at[i], small_r.at[i])

    stage[...] = recv_small[...].astype(F32).reshape(GROUPS * 16, 128)
    for k in range(3 * TPG):
        ag_buf[z, pl.ds(32 * k, 32), :] = stage[pl.ds(k, GROUPS, stride=16), :].astype(BF16)

    for way in (0, 1):
        for p in range(PIECES):
            send_ag(way, 1, p)
    spread(z)

    ways = [(way, d) for d in range(1, HALF + 1) for way in (0, 1) if d <= w_reach(way)]

    def at(d):
        return [w for w in ways if w[1] == d]

    for t in range(1, HALF + 5):
        for way, d in at(t):
            ref = w_slice(w_block(way, d))
            arrive(ref, wz_s.at[way, d - 1], wz_r.at[way, d - 1])
            if d < w_reach(way):
                send_z(way, d + 1)
            start_phase(way, 1, d)
        for way, d in at(t - 1):
            pass_on(way, 1, d)
        for way, d in at(t):
            get_ag(way, d)
        for way, d in at(t - 1):
            end_phase(way, 1, d)
            start_phase(way, 2, d)
        for way, d in at(t):
            spread(w_block(way, d))
        for way, d in at(t - 2):
            pass_on(way, 2, d)
        for way, d in at(t - 3):
            end_phase(way, 2, d)
            start_die(way, d)

    tok_copy.wait()
    teach_copy.wait()
    seq0 = seq_ref[0]
    seq1 = seq_ref[1]
    upper = iota((TOK, 128), 0) < SEQ_LEN
    slot_of = jnp.where(upper, seq0, seq1)
    chosen = slot_of == iota((TOK, 128), 1) // R
    low_all = jnp.zeros((TOK, 128), F32)
    for k in range(8):
        low_all = low_all + dot(
            tok_buf[:, 640 * k : 640 * (k + 1)], tall[pl.ds(640 * k, 640), :].astype(BF16)
        )
    low = jnp.where(chosen, low_all * SHRINK, 0.0).astype(BF16)
    for slot in range(TPG):
        for k in range(8):
            b_mat[pl.ds(32 * slot, 32), 128 * k : 128 * (k + 1)] = low_rows[
                slot, pl.ds(128 + k, 32, stride=8), :
            ].astype(BF16)

    lane = iota((1, GROUPS), 1)
    own_first = jnp.sum(jnp.where(lane < dp, share, 0.0), axis=1, keepdims=True)
    counts = counts_ref[...].astype(F32)
    weights = (jnp.sum(counts, axis=1, keepdims=True) / TASKS) / counts
    task_lane = iota((1, TASKS), 1).astype(F32)

    def weight_of(slot):
        hit = task_lane == own_first + slot.astype(F32)
        return jnp.sum(jnp.where(hit, weights, 0.0), axis=1, keepdims=True) * LOSS_SCALE

    weight0 = weight_of(seq0)
    weight1 = weight_of(seq1)

    for q in range(SIDE):
        cols = pl.ds(256 * q, 256)
        acc[:, cols] = dot(low, b_mat[:, cols]) * RANK_SCALE - teach_buf[:, cols].astype(F32)

    for way, d in ways:
        end_die(way, d)

    for q in range(SIDE):
        cols = pl.ds(256 * q, 256)

        def body(k, total):
            rows = pl.ds(pl.multiple_of(640 * k, 128), 640)
            wide = jnp.concatenate([w_buf[q, 0, rows, :], w_buf[q, 1, rows, :]], axis=1)
            return total + dot(tok_buf[:, rows], wide)

        total = lax.fori_loop(0, 8, body, acc[:, cols])
        acc[:SEQ_LEN, cols] = total[:SEQ_LEN] * weight0
        acc[SEQ_LEN:, cols] = total[SEQ_LEN:] * weight1

    grad = acc[...].astype(BF16)
    low_grad = lax.dot_general(
        grad, b_mat[...], (((1,), (1,)), ((), ())), preferred_element_type=F32
    )
    low_grad = jnp.where(chosen, low_grad * RANK_SCALE, 0.0).astype(BF16)
    for k in range(8):
        tall[pl.ds(640 * k, 640), :] = (
            lax.dot_general(
                tok_buf[:, 640 * k : 640 * (k + 1)],
                low_grad,
                (((0,), (0,)), ((), ())),
                preferred_element_type=F32,
            )
            * SHRINK
        )
    tall[pl.ds(D, TALL - D), :] = jnp.zeros((TALL - D, 128), F32)
    second = (
        lax.dot_general(low, grad, (((0,), (0,)), ((), ())), preferred_element_type=F32)
        * RANK_SCALE
    )
    for slot in range(TPG):
        low_rows[slot, pl.ds(0, 128), :] = jnp.zeros((128, 128), F32)
        for k in range(8):
            low_rows[slot, pl.ds(128 + k, 32, stride=8), :] = second[
                32 * slot : 32 * (slot + 1), 128 * k : 128 * (k + 1)
            ]

    def collect(m):
        parts = [
            jnp.concatenate(
                [
                    tall[pl.ds(12 * m + 4 * s + j, GROUPS, stride=192), :].astype(BF16)
                    for j in range(4)
                ],
                axis=1,
            )
            for s in range(3)
        ]
        moved = dot(jnp.concatenate(parts, axis=0), perm_buf[...])
        for slot in range(TPG):
            for s in range(3):
                from_a = moved[32 * s : 32 * (s + 1), 128 * slot : 128 * (slot + 1)]
                from_b = low_rows[slot, pl.ds(3 * m + s, 8, stride=48), :]
                flat = 48 * (iota((8, 128), 0) + 24) + 3 * m + s
                tail = jnp.where(flat >= D * R // 128, from_b, from_a[24:])
                own[m, pl.ds(96 * slot + 32 * s, 32), :] = jnp.concatenate(
                    [from_a[:24], tail], axis=0
                ).astype(BF16)

    def rs_dest(way, k):
        return wrap(z + f * (HALF - k) if way == 0 else z - f * (HALF - 1 - k), MEMBERS)

    for k in range(HALF):
        for way in (0, 1):
            if k >= w_reach(way):
                continue
            m = rs_dest(way, k)
            collect(m)
            for p in range(PIECES):
                rows = pl.ds(p * PIECE, PIECE)
                if k == 0:
                    src = own.at[m, rows, :]
                else:
                    arrive(
                        recv_run.at[way, k - 1, rows, :],
                        rs_s.at[way, k - 1, p],
                        rs_r.at[way, k - 1, p],
                    )
                    send_run[way, k, rows, :] = (
                        recv_run[way, k - 1, rows, :].astype(F32) + own[m, rows, :].astype(F32)
                    ).astype(BF16)
                    src = send_run.at[way, k, rows, :]
                send(
                    src,
                    recv_run.at[way, k, rows, :],
                    rs_s.at[way, k, p],
                    rs_r.at[way, k, p],
                    dp,
                    z_to(way),
                )
    collect(z)
    for p in range(PIECES):
        rows = pl.ds(p * PIECE, PIECE)
        for way in (0, 1):
            k = w_reach(way) - 1
            arrive(recv_run.at[way, k, rows, :], rs_s.at[way, k, p], rs_r.at[way, k, p])
        stage[rows, :] = (
            recv_run[0, HALF - 1, rows, :].astype(F32)
            + recv_run[1, HALF - 2, rows, :].astype(F32)
            + own[z, rows, :].astype(F32)
        )
    stage[pl.ds(ROWS, 128), :] = jnp.zeros((128, 128), F32)

    @pl.loop(0, GROUPS)
    def _(g):
        send_back[g] = stage[pl.ds(g, 16, stride=GROUPS), :].astype(BF16)

    @pl.loop(1, GROUPS)
    def _(i):
        to = lax.rem(dp + i, GROUPS)
        remote(send_back.at[to], recv_back.at[dp], back_s.at[i], back_r.at[i], to, z).start()

    recv_back[dp] = send_back[dp]

    @pl.loop(1, GROUPS)
    def _(i):
        frm = wrap(dp - i, GROUPS)
        arrive(recv_back.at[frm], back_s.at[i], back_r.at[i])

    stage[...] = recv_back[...].astype(F32).reshape(GROUPS * 16, 128)
    for s in range(3):
        sums = jnp.concatenate(
            [stage[pl.ds(slot * 3 + s, GROUPS, stride=16), :] for slot in range(TPG)], axis=0
        ).astype(BF16)
        out_ref[:, 128 * s : 128 * (s + 1)] = lax.dot_general(
            codes_sel, sums, (((0,), (0,)), ((), ())), preferred_element_type=F32
        )

    for copy in sent:
        copy.wait_send()

    @pl.loop(1, GROUPS)
    def _(i):
        to = lax.rem(dp + i, GROUPS)
        remote(
            send_small.at[to], recv_small.at[dp], small_s.at[i], small_r.at[i], to, z
        ).wait_send()
        remote(
            send_back.at[to], recv_back.at[dp], back_s.at[i], back_r.at[i], to, z
        ).wait_send()


def shards(
    task_codes, hyper_weight, frozen_weight, tokens, teacher, seq_slot, task_share, token_counts
):
    vmem = pl.BlockSpec(memory_space=pltpu.VMEM)
    smem = pl.BlockSpec(memory_space=pltpu.SMEM)
    hbm = pl.BlockSpec(memory_space=pl.ANY)
    dma = pltpu.SemaphoreType.DMA
    small = pltpu.VMEM((GROUPS, 16, 128), BF16)
    return pl.pallas_call(
        step_kernel,
        out_shape=jax.ShapeDtypeStruct((128, 384), F32),
        in_specs=[vmem, vmem, hbm, hbm, hbm, smem, vmem, vmem],
        out_specs=vmem,
        scratch_shapes=[
            pltpu.VMEM((SIDE, 2, D, 128), BF16),
            pltpu.VMEM((TOK, D), BF16),
            pltpu.VMEM((TOK, KV), BF16),
            pltpu.VMEM((512, 512), BF16),
            pltpu.VMEM((512, 128), F32),
            small,
            small,
            small,
            small,
            pltpu.VMEM((MEMBERS, ROWS, 128), BF16),
            pltpu.VMEM((TALL, 128), F32),
            pltpu.VMEM((TPG, ROWS, 128), F32),
            pltpu.VMEM((128, KV), BF16),
            pltpu.VMEM((TOK, KV), F32),
            pltpu.VMEM((MEMBERS, ROWS, 128), BF16),
            pltpu.VMEM((2, HALF, ROWS, 128), BF16),
            pltpu.VMEM((2, HALF, ROWS, 128), BF16),
            dma((10,)),
            dma((GROUPS,)),
            dma((GROUPS,)),
            dma((GROUPS,)),
            dma((GROUPS,)),
            dma((2, HALF)),
            dma((2, HALF)),
            dma((2, HALF, 3)),
            dma((2, HALF, 3)),
            dma((2, HALF, 3)),
            dma((2, HALF, 3)),
            dma((2, HALF)),
            dma((2, HALF)),
            dma((2, HALF, PIECES)),
            dma((2, HALF, PIECES)),
            dma((2, HALF, PIECES)),
            dma((2, HALF, PIECES)),
        ],
        compiler_params=pltpu.CompilerParams(collective_id=0, has_side_effects=True),
    )(
        task_codes,
        hyper_weight,
        frozen_weight,
        tokens,
        teacher,
        seq_slot,
        task_share.reshape(1, -1),
        token_counts.reshape(1, -1),
    )


def solution(mesh):
    placed = (
        P(),
        P(None, ("dp", "mp")),
        P("mp", None),
        P(("dp", "mp"), None),
        P(("dp", "mp"), None),
        P(("dp", "mp")),
        P(),
        P(),
    )
    return jax.shard_map(
        shards, mesh=mesh, in_specs=placed, out_specs=P(None, ("dp", "mp")), check_vma=False
    )
```

time: 365 us -> 130 us (0.36)
  the two profiles are of different devices: /device:TPU:2 before, /device:TPU:1 now
where the time goes in v1:
time: 130 us
  Pallas kernels  128 us (98%)
  local copies, waits for them, and re-layouts  1.62 us (1%)
    pallas_call x1, Pallas kernels, shards(): pl.pallas_call(step_kernel, out_shape=jax.ShapeDtypeStruct((128, 384), F3...  128 us

profile of v1, /device:TPU:1, one launch (start us, length us, event | category | flops | bytes accessed | tf_op | source)
XLA Modules:
  0.0 129.7 jit_solution(6219857743652365472)
XLA Ops:
  0.0 128.1 %shard_map.82 = f32[128,384]{1,0:T(8,128)} custom-call(bf16[64,128]{1,0:T(8,128)(2,1)} %codes_ref.1, bf16[128,384]{1,0:T(8,128)(2,1)} %hyper_ref.1, bf16[320,1024]{1,0:T(8,128)(2,1)} %frozen_hbm.1, bf16[256,5120]{1,0:T(8,128)(2,1)} %tokens_hbm.1, bf16[256,1024]{1,0:T(8,128)(2,1)} %teacher_hbm.1, s32[2]{0:T(128)} %seq_ref.1, s32[1,32]{1,0:T(1,128)} %bitcast.2, ...), custom_call_target="tpu_custom_call" | custom-call | tf_op jit(solution)/shard_map/pallas_call | solution.py:529
  128.1 1.6 %copy.10 = f32[128,384]{1,0:T(8,128)} copy(f32[128,384]{1,0:T(8,128)} %shard_map.82) | data formatting | bytes 393216

commit v2 on v1

--- a/solution.py
+++ b/solution.py
@@ -22,6 +22,8 @@
 ROWS = 3 * TPG * GROUPS
 PIECES = 2
 PIECE = ROWS // PIECES
+RS_PIECES = 4
+RS_PIECE = ROWS // RS_PIECES
 HALF = MEMBERS // 2
 TALL = 192 * GROUPS
 MESH = pl.DeviceIdType.MESH
@@ -53,6 +55,9 @@
     w_buf,
     tok_buf,
     teach_buf,
+    tok_blocks,
+    tok_t,
+    grad_buf,
     perm_buf,
     stage,
     send_small,
@@ -166,25 +171,10 @@
                 slot * GROUPS : (slot + 1) * GROUPS
             ]
 
-    @pl.loop(0, GROUPS)
-    def _(g):
+    for g in range(GROUPS):
         send_small[g] = stage[pl.ds(g, 16, stride=GROUPS), :].astype(BF16)
 
-    row = iota((512, 512), 0)
-    target = lax.rem(row // 32, 4) * 128 + (row // 128) * 32 + lax.rem(row, 32)
-    perm_buf[...] = jnp.where(iota((512, 512), 1) == target, 1.0, 0.0).astype(BF16)
-
     pl.semaphore_wait(barrier, GROUPS + 1)
-
-    @pl.loop(1, GROUPS)
-    def _(i):
-        to = lax.rem(dp + i, GROUPS)
-        remote(
-            send_small.at[to], recv_small.at[dp], small_s.at[i], small_r.at[i], to, z
-        ).start()
-
-    for copy in local:
-        copy.wait()
 
     def w_block(way, d):
         return wrap(z - f * d if way == 0 else z + f * d, MEMBERS)
@@ -222,44 +212,64 @@
         ref = w_slice(w_block(way, d - 1))
         send(ref, ref, wz_s.at[way, d - 1], wz_r.at[way, d - 1], dp, z_to(way))
 
-    def start_phase(way, phase, d):
-        sems, semr = (p1_s, p1_r) if phase == 1 else (p2_s, p2_r)
-        ref = w_piece(way, phase, w_block(way, d), along(way, phase))
-        send(ref, ref, sems.at[way, d - 1, 0], semr.at[way, d - 1, 0], shifted(way, phase, f), z)
-        send(ref, ref, sems.at[way, d - 1, 1], semr.at[way, d - 1, 1], shifted(way, phase, -f), z)
-
-    def pass_on(way, phase, d):
-        sems, semr = (p1_s, p1_r) if phase == 1 else (p2_s, p2_r)
-        ref = w_piece(way, phase, w_block(way, d), wrap(along(way, phase) - f, SIDE))
-        arrive(ref, sems.at[way, d - 1, 0], semr.at[way, d - 1, 0])
-        send(ref, ref, sems.at[way, d - 1, 2], semr.at[way, d - 1, 2], shifted(way, phase, f), z)
-
-    def end_phase(way, phase, d):
-        sems, semr = (p1_s, p1_r) if phase == 1 else (p2_s, p2_r)
-        zb = w_block(way, d)
-        at = along(way, phase)
-        arrive(
-            w_piece(way, phase, zb, wrap(at + f, SIDE)),
-            sems.at[way, d - 1, 1],
-            semr.at[way, d - 1, 1],
-        )
-        arrive(
-            w_piece(way, phase, zb, wrap(at - 2 * f, SIDE)),
-            sems.at[way, d - 1, 2],
-            semr.at[way, d - 1, 2],
-        )
-
-    def die_part(way, d, core):
-        return w_buf.at[:, core, w_rows(BLK * w_block(way, d), BLK), :]
-
-    def start_die(way, d):
-        ref = die_part(way, d, c)
-        send(ref, ref, die_s.at[way, d - 1], die_r.at[way, d - 1], dp + f, z)
-
-    def end_die(way, d):
-        other = wrap(z + f * d if way == 0 else z - f * d, MEMBERS)
-        ref = w_buf.at[:, 1 - c, w_rows(BLK * other, BLK), :]
-        arrive(ref, die_s.at[way, d - 1], die_r.at[way, d - 1])
+    def sems_of(phase, way, d, kind):
+        if phase == 1:
+            return p1_s.at[way, d - 1, kind], p1_r.at[way, d - 1, kind]
+        return p2_s.at[way, d - 1, kind], p2_r.at[way, d - 1, kind]
+
+    def plane_send(way, phase, d, frm, kind, by):
+        ref = w_piece(way, phase, w_block(way, d), wrap(along(way, phase) + frm, SIDE))
+        send(ref, ref, *sems_of(phase, way, d, kind), shifted(way, phase, by), z)
+
+    def plane_wait(way, phase, d, frm, kind):
+        ref = w_piece(way, phase, w_block(way, d), wrap(along(way, phase) + frm, SIDE))
+        arrive(ref, *sems_of(phase, way, d, kind))
+
+    def twin_send(way, d, frm, kind):
+        ref = w_piece(way, 2, w_block(way, d), wrap(along(way, 2) + frm, SIDE))
+        send(ref, ref, die_s.at[way, d - 1, kind], die_r.at[way, d - 1, kind], dp + f, z)
+
+    def twin_block(way, d):
+        return wrap(z + f * d if way == 0 else z - f * d, MEMBERS)
+
+    def twin_wait(way, d):
+        zb = twin_block(way, d)
+        at_twin = along(way, 2)
+        for kind, frm in enumerate((0, -f, f, -2 * f)):
+            i = wrap(at_twin + (frm if kind == 0 else -frm), SIDE)
+            if way == 0:
+                ref = w_buf.at[i, 1 - c, w_rows(BLK * zb, BLK), :]
+            else:
+                ref = w_buf.at[:, 1 - c, w_rows(BLK * zb + SLICE * i, SLICE), :]
+            arrive(ref, die_s.at[way, d - 1, kind], die_r.at[way, d - 1, kind])
+
+    def take_z(way, d):
+        ref = w_slice(w_block(way, d))
+        arrive(ref, wz_s.at[way, d - 1], wz_r.at[way, d - 1])
+        if d < w_reach(way):
+            send_z(way, d + 1)
+        plane_send(way, 1, d, 0, 0, f)
+        plane_send(way, 1, d, 0, 1, -f)
+        plane_send(way, 1, d, 0, 2, 2 * f)
+
+    def start_second(way, d):
+        plane_wait(way, 1, d, -f, 0)
+        plane_wait(way, 1, d, f, 1)
+        plane_wait(way, 1, d, -2 * f, 2)
+        plane_send(way, 2, d, 0, 0, f)
+        plane_send(way, 2, d, 0, 1, -f)
+        twin_send(way, d, 0, 0)
+
+    def relay_second(way, d):
+        plane_wait(way, 2, d, -f, 0)
+        plane_send(way, 2, d, -f, 2, f)
+        twin_send(way, d, -f, 1)
+
+    def end_second(way, d):
+        plane_wait(way, 2, d, f, 1)
+        twin_send(way, d, f, 2)
+        plane_wait(way, 2, d, -2 * f, 2)
+        twin_send(way, d, -2 * f, 3)
 
     def ag_piece(way, d, p):
         return ag_buf.at[w_block(way, d), pl.ds(p * PIECE, PIECE), :]
@@ -289,8 +299,29 @@
                 last = ag_buf[m, pl.ds(96 * slot + 32 * s + 16, 16), :].astype(F32)
                 low_rows[slot, pl.ds(3 * m + s, 8, stride=48), :] = last[8:16]
 
+    for copy in local:
+        copy.wait()
     for way in (0, 1):
         send_z(way, 1)
+
+    @pl.loop(1, GROUPS)
+    def _(i):
+        to = lax.rem(dp + i, GROUPS)
+        remote(
+            send_small.at[to], recv_small.at[dp], small_s.at[i], small_r.at[i], to, z
+        ).start()
+
+    row = iota((512, 512), 0)
+    target = ((row >> 5) & 3) * 128 + (row >> 7) * 32 + (row & 31)
+    perm_buf[...] = jnp.where(iota((512, 512), 1) == target, 1.0, 0.0).astype(BF16)
+
+    ways = [(way, d) for d in range(1, HALF + 1) for way in (0, 1) if d <= w_reach(way)]
+
+    def at(d):
+        return [w for w in ways if w[1] == d]
+
+    for way, d in at(1):
+        take_z(way, d)
 
     recv_small[dp] = send_small[dp]
 
@@ -308,35 +339,61 @@
             send_ag(way, 1, p)
     spread(z)
 
-    ways = [(way, d) for d in range(1, HALF + 1) for way in (0, 1) if d <= w_reach(way)]
-
-    def at(d):
-        return [w for w in ways if w[1] == d]
-
-    for t in range(1, HALF + 5):
-        for way, d in at(t):
-            ref = w_slice(w_block(way, d))
-            arrive(ref, wz_s.at[way, d - 1], wz_r.at[way, d - 1])
-            if d < w_reach(way):
-                send_z(way, d + 1)
-            start_phase(way, 1, d)
-        for way, d in at(t - 1):
-            pass_on(way, 1, d)
-        for way, d in at(t):
-            get_ag(way, d)
-        for way, d in at(t - 1):
-            end_phase(way, 1, d)
-            start_phase(way, 2, d)
-        for way, d in at(t):
-            spread(w_block(way, d))
-        for way, d in at(t - 2):
-            pass_on(way, 2, d)
-        for way, d in at(t - 3):
-            end_phase(way, 2, d)
-            start_die(way, d)
+    def frozen(blocks):
+        @pl.loop(0, SIDE)
+        def _(q):
+            cols = pl.ds(pl.multiple_of(256 * q, 256), 256)
+            total = None
+            for zb in blocks:
+                rows = w_rows(BLK * zb, BLK)
+                wide = jnp.concatenate([w_buf[q, 0, rows, :], w_buf[q, 1, rows, :]], axis=1)
+                part = dot(tok_blocks[zb], wide)
+                total = part if total is None else total + part
+            acc[:, cols] = acc[:, cols] + total
+
+    def prepare(k):
+        for zb in (2 * k, 2 * k + 1):
+            tok_blocks[zb] = tok_buf[:, BLK * zb : BLK * (zb + 1)]
+        tok_t[pl.ds(2 * BLK * k, 2 * BLK), :] = tok_buf[:, 2 * BLK * k : 2 * BLK * (k + 1)].T
 
     tok_copy.wait()
     teach_copy.wait()
+
+    def steps(t):
+        for way, d in at(t):
+            take_z(way, d)
+        for way, d in at(t - 1):
+            start_second(way, d)
+        for way, d in at(t - 2):
+            relay_second(way, d)
+        for way, d in at(t - 3):
+            end_second(way, d)
+
+    def finish(t):
+        for way, d in at(t):
+            twin_wait(way, d)
+        frozen([w_block(way, d) for way, d in at(t)])
+
+    for t in range(2, HALF + 1):
+        steps(t)
+        for way, d in at(t - 1):
+            get_ag(way, d)
+        if t <= 5:
+            prepare(2 * (t - 2))
+            prepare(2 * (t - 2) + 1)
+        for way, d in at(t - 1):
+            spread(w_block(way, d))
+        if t == 5:
+            acc[...] = -teach_buf[...].astype(F32)
+            frozen([z])
+        if t > 5:
+            finish(t - 5)
+    steps(HALF + 1)
+    for way, d in at(HALF):
+        get_ag(way, d)
+        spread(w_block(way, d))
+    finish(HALF - 4)
+
     seq0 = seq_ref[0]
     seq1 = seq_ref[1]
     upper = iota((TOK, 128), 0) < SEQ_LEN
@@ -367,40 +424,27 @@
     weight0 = weight_of(seq0)
     weight1 = weight_of(seq1)
 
+    steps(HALF + 2)
     for q in range(SIDE):
         cols = pl.ds(256 * q, 256)
-        acc[:, cols] = dot(low, b_mat[:, cols]) * RANK_SCALE - teach_buf[:, cols].astype(F32)
-
-    for way, d in ways:
-        end_die(way, d)
-
+        acc[:, cols] = acc[:, cols] + dot(low, b_mat[:, cols]) * RANK_SCALE
+    finish(HALF - 3)
+    finish(HALF - 2)
+    steps(HALF + 3)
+    finish(HALF - 1)
+    finish(HALF)
     for q in range(SIDE):
         cols = pl.ds(256 * q, 256)
-
-        def body(k, total):
-            rows = pl.ds(pl.multiple_of(640 * k, 128), 640)
-            wide = jnp.concatenate([w_buf[q, 0, rows, :], w_buf[q, 1, rows, :]], axis=1)
-            return total + dot(tok_buf[:, rows], wide)
-
-        total = lax.fori_loop(0, 8, body, acc[:, cols])
-        acc[:SEQ_LEN, cols] = total[:SEQ_LEN] * weight0
-        acc[SEQ_LEN:, cols] = total[SEQ_LEN:] * weight1
-
-    grad = acc[...].astype(BF16)
+        grad_buf[:SEQ_LEN, cols] = (acc[:SEQ_LEN, cols] * weight0).astype(BF16)
+        grad_buf[SEQ_LEN:, cols] = (acc[SEQ_LEN:, cols] * weight1).astype(BF16)
+
+    grad = grad_buf[...]
     low_grad = lax.dot_general(
         grad, b_mat[...], (((1,), (1,)), ((), ())), preferred_element_type=F32
     )
     low_grad = jnp.where(chosen, low_grad * RANK_SCALE, 0.0).astype(BF16)
     for k in range(8):
-        tall[pl.ds(640 * k, 640), :] = (
-            lax.dot_general(
-                tok_buf[:, 640 * k : 640 * (k + 1)],
-                low_grad,
-                (((0,), (0,)), ((), ())),
-                preferred_element_type=F32,
-            )
-            * SHRINK
-        )
+        tall[pl.ds(640 * k, 640), :] = dot(tok_t[pl.ds(640 * k, 640), :], low_grad) * SHRINK
     tall[pl.ds(D, TALL - D), :] = jnp.zeros((TALL - D, 128), F32)
     second = (
         lax.dot_general(low, grad, (((0,), (0,)), ((), ())), preferred_element_type=F32)
@@ -438,37 +482,41 @@
     def rs_dest(way, k):
         return wrap(z + f * (HALF - k) if way == 0 else z - f * (HALF - 1 - k), MEMBERS)
 
-    for k in range(HALF):
-        for way in (0, 1):
-            if k >= w_reach(way):
-                continue
-            m = rs_dest(way, k)
-            collect(m)
-            for p in range(PIECES):
-                rows = pl.ds(p * PIECE, PIECE)
-                if k == 0:
-                    src = own.at[m, rows, :]
-                else:
-                    arrive(
-                        recv_run.at[way, k - 1, rows, :],
-                        rs_s.at[way, k - 1, p],
-                        rs_r.at[way, k - 1, p],
-                    )
-                    send_run[way, k, rows, :] = (
-                        recv_run[way, k - 1, rows, :].astype(F32) + own[m, rows, :].astype(F32)
-                    ).astype(BF16)
-                    src = send_run.at[way, k, rows, :]
-                send(
-                    src,
-                    recv_run.at[way, k, rows, :],
-                    rs_s.at[way, k, p],
-                    rs_r.at[way, k, p],
-                    dp,
-                    z_to(way),
+    def run_send(way, k, p, src):
+        send(
+            src,
+            recv_run.at[way, k, pl.ds(p * RS_PIECE, RS_PIECE), :],
+            rs_s.at[way, k, p],
+            rs_r.at[way, k, p],
+            dp,
+            z_to(way),
+        )
+
+    for way in (0, 1):
+        m = rs_dest(way, 0)
+        collect(m)
+        for p in range(RS_PIECES):
+            run_send(way, 0, p, own.at[m, pl.ds(p * RS_PIECE, RS_PIECE), :])
+    for k in range(1, HALF):
+        live = [way for way in (0, 1) if k < w_reach(way)]
+        for way in live:
+            collect(rs_dest(way, k))
+        for p in range(RS_PIECES):
+            rows = pl.ds(p * RS_PIECE, RS_PIECE)
+            for way in live:
+                arrive(
+                    recv_run.at[way, k - 1, rows, :],
+                    rs_s.at[way, k - 1, p],
+                    rs_r.at[way, k - 1, p],
                 )
+                send_run[way, k, rows, :] = (
+                    recv_run[way, k - 1, rows, :].astype(F32)
+                    + own[rs_dest(way, k), rows, :].astype(F32)
+                ).astype(BF16)
+                run_send(way, k, p, send_run.at[way, k, rows, :])
     collect(z)
-    for p in range(PIECES):
-        rows = pl.ds(p * PIECE, PIECE)
+    for p in range(RS_PIECES):
+        rows = pl.ds(p * RS_PIECE, RS_PIECE)
         for way in (0, 1):
             k = w_reach(way) - 1
             arrive(recv_run.at[way, k, rows, :], rs_s.at[way, k, p], rs_r.at[way, k, p])
@@ -479,8 +527,7 @@
         )
     stage[pl.ds(ROWS, 128), :] = jnp.zeros((128, 128), F32)
 
-    @pl.loop(0, GROUPS)
-    def _(g):
+    for g in range(GROUPS):
         send_back[g] = stage[pl.ds(g, 16, stride=GROUPS), :].astype(BF16)
 
     @pl.loop(1, GROUPS)
@@ -534,6 +581,9 @@
         scratch_shapes=[
             pltpu.VMEM((SIDE, 2, D, 128), BF16),
             pltpu.VMEM((TOK, D), BF16),
+            pltpu.VMEM((TOK, KV), BF16),
+            pltpu.VMEM((MEMBERS, TOK, BLK), BF16),
+            pltpu.VMEM((D, TOK), BF16),
             pltpu.VMEM((TOK, KV), BF16),
             pltpu.VMEM((512, 512), BF16),
             pltpu.VMEM((512, 128), F32),
@@ -560,12 +610,12 @@
             dma((2, HALF, 3)),
             dma((2, HALF, 3)),
             dma((2, HALF, 3)),
-            dma((2, HALF)),
-            dma((2, HALF)),
+            dma((2, HALF, 4)),
+            dma((2, HALF, 4)),
             dma((2, HALF, PIECES)),
             dma((2, HALF, PIECES)),
-            dma((2, HALF, PIECES)),
-            dma((2, HALF, PIECES)),
+            dma((2, HALF, RS_PIECES)),
+            dma((2, HALF, RS_PIECES)),
         ],
         compiler_params=pltpu.CompilerParams(collective_id=0, has_side_effects=True),
     )(

time: 130 us -> 106 us (0.82)
  Pallas kernels: 128 us -> 104 us
    pallas_call x1, Pallas kernels: 128 us -> 104 us  [shards(): pl.pallas_call(step_kernel, out_shape=jax.ShapeDtypeStruct((128, 384), F3...]
where the time goes in v2:
time: 106 us
  Pallas kernels  104 us (98%)
  local copies, waits for them, and re-layouts  1.62 us (2%)
    pallas_call x1, Pallas kernels, shards(): pl.pallas_call(step_kernel, out_shape=jax.ShapeDtypeStruct((128, 384), F3...  104 us

profile of v2, /device:TPU:1, one launch (start us, length us, event | category | flops | bytes accessed | tf_op | source)
XLA Modules:
  0.0 106.1 jit_solution(7607717100667314260)
XLA Ops:
  0.0 104.5 %shard_map.82 = f32[128,384]{1,0:T(8,128)} custom-call(bf16[64,128]{1,0:T(8,128)(2,1)} %codes_ref.1, bf16[128,384]{1,0:T(8,128)(2,1)} %hyper_ref.1, bf16[320,1024]{1,0:T(8,128)(2,1)} %frozen_hbm.1, bf16[256,5120]{1,0:T(8,128)(2,1)} %tokens_hbm.1, bf16[256,1024]{1,0:T(8,128)(2,1)} %teacher_hbm.1, s32[2]{0:T(128)} %seq_ref.1, s32[1,32]{1,0:T(1,128)} %bitcast.2, ...), custom_call_target="tpu_custom_call" | custom-call | tf_op jit(solution)/shard_map/pallas_call | solution.py:576
  104.5 1.6 %copy.10 = f32[128,384]{1,0:T(8,128)} copy(f32[128,384]{1,0:T(8,128)} %shard_map.82) | data formatting | bytes 393216

commit v3 on v2

--- a/solution.py
+++ b/solution.py
@@ -20,7 +20,7 @@
 BLK = D // MEMBERS
 SLICE = BLK // SIDE
 ROWS = 3 * TPG * GROUPS
-PIECES = 2
+PIECES = 4
 PIECE = ROWS // PIECES
 RS_PIECES = 4
 RS_PIECE = ROWS // RS_PIECES
@@ -34,6 +34,18 @@
 RANK_SCALE = 1.0 / math.sqrt(R)
 
 
+PLANE = sorted(
+    (
+        (dy, dx, dc)
+        for dy in range(SIDE)
+        for dx in range(SIDE)
+        for dc in range(2)
+        if dy or dx or dc
+    ),
+    key=lambda o: (-min(o[0], SIDE - o[0]) - min(o[1], SIDE - o[1]), o),
+)
+
+
 def dot(a, b):
     return jnp.dot(a, b, preferred_element_type=F32)
 
@@ -43,8 +55,8 @@
 
 
 def step_kernel(
-    codes_ref,
-    hyper_ref,
+    codes_hbm,
+    hyper_hbm,
     frozen_hbm,
     tokens_hbm,
     teacher_hbm,
@@ -52,6 +64,8 @@
     share_ref,
     counts_ref,
     out_ref,
+    codes_ref,
+    hyper_ref,
     w_buf,
     tok_buf,
     teach_buf,
@@ -73,21 +87,14 @@
     send_run,
     recv_run,
     local_sem,
-    small_s,
     small_r,
-    back_s,
     back_r,
-    wz_s,
+    out_s,
     wz_r,
-    p1_s,
     p1_r,
-    p2_s,
     p2_r,
-    die_s,
     die_r,
-    ag_s,
     ag_r,
-    rs_s,
     rs_r,
 ):
     dp = lax.axis_index("dp")
@@ -113,23 +120,31 @@
             device_id_type=MESH,
         )
 
-    sent = []
+    small_s, back_s, wz_s, p1_s, p2_s, die_s, ag_s, rs_s = (out_s.at[i] for i in range(8))
 
     def send(src, dst, ssem, rsem, to_dp, to_z):
-        copy = remote(src, dst, ssem, rsem, to_dp, to_z)
-        copy.start()
-        sent.append(copy)
-
-    def arrive(dst, ssem, rsem):
-        remote(dst, dst, ssem, rsem, dp, z).wait_recv()
+        remote(src, dst, ssem, rsem, to_dp, to_z).start()
+
+    def arrive(dst, rsem):
+        remote(dst, dst, out_s.at[0], rsem, dp, z).wait_recv()
+
+    def all_sent(like, ssem):
+        remote(like, like, ssem, small_r, dp, z).wait_send()
+
+    codes_copy = pltpu.make_async_copy(codes_hbm, codes_ref, local_sem.at[3])
+    hyper_copy = pltpu.make_async_copy(hyper_hbm, hyper_ref, local_sem.at[4])
+    codes_copy.start()
+    hyper_copy.start()
 
     barrier = pltpu.get_barrier_semaphore()
 
-    @pl.loop(1, GROUPS)
-    def _(i):
-        pl.semaphore_signal(
-            barrier, inc=1, device_id=(lax.rem(dp + i, GROUPS), z), device_id_type=MESH
-        )
+    def peer(offset, sign):
+        dy, dx, dc = offset
+        core = c if dc == 0 else 1 - c
+        return (wrap(y + sign * dy, SIDE) * SIDE + wrap(x + sign * dx, SIDE)) * 2 + core
+
+    for offset in PLANE:
+        pl.semaphore_signal(barrier, inc=1, device_id=(peer(offset, 1), z), device_id_type=MESH)
 
     for shift in (1, -1):
         pl.semaphore_signal(
@@ -143,11 +158,11 @@
                 pltpu.make_async_copy(
                     frozen_hbm.at[:, pl.ds((2 * yy + cc) * 128, 128)],
                     w_buf.at[yy, cc, pl.ds(pl.multiple_of(BLK * z, 16), BLK), :],
-                    local_sem.at[2 * yy + cc],
+                    local_sem.at[0],
                 )
             )
-    tok_copy = pltpu.make_async_copy(tokens_hbm, tok_buf, local_sem.at[8])
-    teach_copy = pltpu.make_async_copy(teacher_hbm, teach_buf, local_sem.at[9])
+    tok_copy = pltpu.make_async_copy(tokens_hbm, tok_buf, local_sem.at[1])
+    teach_copy = pltpu.make_async_copy(teacher_hbm, teach_buf, local_sem.at[2])
     for copy in local:
         copy.start()
     tok_copy.start()
@@ -162,6 +177,8 @@
     slot_row = (iota((TPG * GROUPS, TASKS), 0) // GROUPS).astype(F32)
     task_col = iota((TPG * GROUPS, TASKS), 1).astype(F32)
     picks = (task_col == first + slot_row) & (slot_row < mine)
+    codes_copy.wait()
+    hyper_copy.wait()
     codes_sel = dot(jnp.where(picks, 1.0, 0.0).astype(BF16), codes_ref[...]).astype(BF16)
     stage[pl.ds(ROWS, 128), :] = jnp.zeros((128, 128), F32)
     for s in range(3):
@@ -210,42 +227,31 @@
 
     def send_z(way, d):
         ref = w_slice(w_block(way, d - 1))
-        send(ref, ref, wz_s.at[way, d - 1], wz_r.at[way, d - 1], dp, z_to(way))
-
-    def sems_of(phase, way, d, kind):
-        if phase == 1:
-            return p1_s.at[way, d - 1, kind], p1_r.at[way, d - 1, kind]
-        return p2_s.at[way, d - 1, kind], p2_r.at[way, d - 1, kind]
+        send(ref, ref, wz_s, wz_r.at[way, d - 1], dp, z_to(way))
 
     def plane_send(way, phase, d, frm, kind, by):
         ref = w_piece(way, phase, w_block(way, d), wrap(along(way, phase) + frm, SIDE))
-        send(ref, ref, *sems_of(phase, way, d, kind), shifted(way, phase, by), z)
-
-    def plane_wait(way, phase, d, frm, kind):
-        ref = w_piece(way, phase, w_block(way, d), wrap(along(way, phase) + frm, SIDE))
-        arrive(ref, *sems_of(phase, way, d, kind))
-
-    def twin_send(way, d, frm, kind):
+        if phase == 1:
+            ssem, rsem = p1_s, p1_r.at[way, d - 1]
+        else:
+            ssem, rsem = p2_s, p2_r.at[way, d - 1, min(kind, 1)]
+        send(ref, ref, ssem, rsem, shifted(way, phase, by), z)
+
+    def twin_send(way, d, frm):
         ref = w_piece(way, 2, w_block(way, d), wrap(along(way, 2) + frm, SIDE))
-        send(ref, ref, die_s.at[way, d - 1, kind], die_r.at[way, d - 1, kind], dp + f, z)
+        send(ref, ref, die_s, die_r.at[way, d - 1], dp + f, z)
 
     def twin_block(way, d):
         return wrap(z + f * d if way == 0 else z - f * d, MEMBERS)
 
     def twin_wait(way, d):
-        zb = twin_block(way, d)
-        at_twin = along(way, 2)
-        for kind, frm in enumerate((0, -f, f, -2 * f)):
-            i = wrap(at_twin + (frm if kind == 0 else -frm), SIDE)
-            if way == 0:
-                ref = w_buf.at[i, 1 - c, w_rows(BLK * zb, BLK), :]
-            else:
-                ref = w_buf.at[:, 1 - c, w_rows(BLK * zb + SLICE * i, SLICE), :]
-            arrive(ref, die_s.at[way, d - 1, kind], die_r.at[way, d - 1, kind])
+        arrive(
+            w_buf.at[:, 1 - c, w_rows(BLK * twin_block(way, d), BLK), :], die_r.at[way, d - 1]
+        )
 
     def take_z(way, d):
         ref = w_slice(w_block(way, d))
-        arrive(ref, wz_s.at[way, d - 1], wz_r.at[way, d - 1])
+        arrive(ref, wz_r.at[way, d - 1])
         if d < w_reach(way):
             send_z(way, d + 1)
         plane_send(way, 1, d, 0, 0, f)
@@ -253,36 +259,34 @@
         plane_send(way, 1, d, 0, 2, 2 * f)
 
     def start_second(way, d):
-        plane_wait(way, 1, d, -f, 0)
-        plane_wait(way, 1, d, f, 1)
-        plane_wait(way, 1, d, -2 * f, 2)
+        arrive(w_buf.at[0, c, pl.ds(0, 3 * SLICE), :], p1_r.at[way, d - 1])
         plane_send(way, 2, d, 0, 0, f)
         plane_send(way, 2, d, 0, 1, -f)
-        twin_send(way, d, 0, 0)
+        twin_send(way, d, 0)
 
     def relay_second(way, d):
-        plane_wait(way, 2, d, -f, 0)
+        arrive(
+            w_piece(way, 2, w_block(way, d), wrap(along(way, 2) - f, SIDE)), p2_r.at[way, d - 1, 0]
+        )
         plane_send(way, 2, d, -f, 2, f)
-        twin_send(way, d, -f, 1)
+        twin_send(way, d, -f)
 
     def end_second(way, d):
-        plane_wait(way, 2, d, f, 1)
-        twin_send(way, d, f, 2)
-        plane_wait(way, 2, d, -2 * f, 2)
-        twin_send(way, d, -2 * f, 3)
+        arrive(w_buf.at[0, c, pl.ds(0, 2 * BLK), :], p2_r.at[way, d - 1, 1])
+        twin_send(way, d, f)
+        twin_send(way, d, -2 * f)
 
     def ag_piece(way, d, p):
         return ag_buf.at[w_block(way, d), pl.ds(p * PIECE, PIECE), :]
 
     def send_ag(way, d, p):
         ref = ag_piece(way, d - 1, p)
-        send(ref, ref, ag_s.at[way, d - 1, p], ag_r.at[way, d - 1, p], dp, z_to(way))
-
-    def get_ag(way, d):
-        for p in range(PIECES):
-            arrive(ag_piece(way, d, p), ag_s.at[way, d - 1, p], ag_r.at[way, d - 1, p])
-            if d < w_reach(way):
-                send_ag(way, d + 1, p)
+        send(ref, ref, ag_s, ag_r.at[way, d - 1, p], dp, z_to(way))
+
+    def get_ag(way, d, p):
+        arrive(ag_piece(way, d, p), ag_r.at[way, d - 1, p])
+        if d < w_reach(way):
+            send_ag(way, d + 1, p)
 
     def spread(m):
         block = jnp.concatenate(
@@ -299,17 +303,20 @@
                 last = ag_buf[m, pl.ds(96 * slot + 32 * s + 16, 16), :].astype(F32)
                 low_rows[slot, pl.ds(3 * m + s, 8, stride=48), :] = last[8:16]
 
-    for copy in local:
-        copy.wait()
+    own_rows = w_buf.at[:, :, w_rows(BLK * z, BLK), :]
+    pltpu.make_async_copy(own_rows, own_rows, local_sem.at[0]).wait()
     for way in (0, 1):
         send_z(way, 1)
 
-    @pl.loop(1, GROUPS)
-    def _(i):
-        to = lax.rem(dp + i, GROUPS)
-        remote(
-            send_small.at[to], recv_small.at[dp], small_s.at[i], small_r.at[i], to, z
-        ).start()
+    def exchange(out, into, ssem, rsem):
+        for offset in PLANE:
+            to = peer(offset, 1)
+            send(out.at[to], into.at[dp], ssem, rsem, to, z)
+
+    def exchanged(into, rsem):
+        arrive(into.at[pl.ds(0, GROUPS - 1)], rsem)
+
+    exchange(send_small, recv_small, small_s, small_r)
 
     row = iota((512, 512), 0)
     target = ((row >> 5) & 3) * 128 + (row >> 7) * 32 + (row & 31)
@@ -319,25 +326,6 @@
 
     def at(d):
         return [w for w in ways if w[1] == d]
-
-    for way, d in at(1):
-        take_z(way, d)
-
-    recv_small[dp] = send_small[dp]
-
-    @pl.loop(1, GROUPS)
-    def _(i):
-        frm = wrap(dp - i, GROUPS)
-        arrive(recv_small.at[frm], small_s.at[i], small_r.at[i])
-
-    stage[...] = recv_small[...].astype(F32).reshape(GROUPS * 16, 128)
-    for k in range(3 * TPG):
-        ag_buf[z, pl.ds(32 * k, 32), :] = stage[pl.ds(k, GROUPS, stride=16), :].astype(BF16)
-
-    for way in (0, 1):
-        for p in range(PIECES):
-            send_ag(way, 1, p)
-    spread(z)
 
     def frozen(blocks):
         @pl.loop(0, SIDE)
@@ -358,41 +346,62 @@
 
     tok_copy.wait()
     teach_copy.wait()
+    for k in range(MEMBERS // 2):
+        prepare(k)
+    acc[...] = -teach_buf[...].astype(F32)
+
+    for way, d in at(1):
+        take_z(way, d)
+
+    recv_small[dp] = send_small[dp]
+
+    exchanged(recv_small, small_r)
+
+    stage[...] = recv_small[...].astype(F32).reshape(GROUPS * 16, 128)
+    for k in range(3 * TPG):
+        ag_buf[z, pl.ds(32 * k, 32), :] = stage[pl.ds(k, GROUPS, stride=16), :].astype(BF16)
+
+    for way in (0, 1):
+        for p in range(PIECES):
+            send_ag(way, 1, p)
+    spread(z)
+
+    frozen([z])
+
+    def get_piece(t, p):
+        for way, d in at(t - 1):
+            get_ag(way, d, p)
 
     def steps(t):
+        get_piece(t, 0)
         for way, d in at(t):
             take_z(way, d)
         for way, d in at(t - 1):
             start_second(way, d)
+        get_piece(t, 1)
+        for way, d in at(t - 3):
+            relay_second(way, d)
+        get_piece(t, 2)
+        for way, d in at(t - 5):
+            end_second(way, d)
         for way, d in at(t - 2):
-            relay_second(way, d)
-        for way, d in at(t - 3):
-            end_second(way, d)
-
-    def finish(t):
-        for way, d in at(t):
+            spread(w_block(way, d))
+        get_piece(t, 3)
+
+    def finish(*distances):
+        blocks = [wd for d in distances for wd in at(d)]
+        for way, d in blocks:
             twin_wait(way, d)
-        frozen([w_block(way, d) for way, d in at(t)])
-
-    for t in range(2, HALF + 1):
+        frozen([w_block(way, d) for way, d in blocks])
+
+    for t in range(2, HALF + 3):
         steps(t)
-        for way, d in at(t - 1):
-            get_ag(way, d)
-        if t <= 5:
-            prepare(2 * (t - 2))
-            prepare(2 * (t - 2) + 1)
-        for way, d in at(t - 1):
-            spread(w_block(way, d))
-        if t == 5:
-            acc[...] = -teach_buf[...].astype(F32)
-            frozen([z])
-        if t > 5:
-            finish(t - 5)
-    steps(HALF + 1)
-    for way, d in at(HALF):
-        get_ag(way, d)
-        spread(w_block(way, d))
-    finish(HALF - 4)
+        if t == 8:
+            finish(1, 2)
+        if t == 10:
+            finish(3, 4)
+
+    steps(HALF + 3)
 
     seq0 = seq_ref[0]
     seq1 = seq_ref[1]
@@ -424,15 +433,14 @@
     weight0 = weight_of(seq0)
     weight1 = weight_of(seq1)
 
-    steps(HALF + 2)
     for q in range(SIDE):
         cols = pl.ds(256 * q, 256)
         acc[:, cols] = acc[:, cols] + dot(low, b_mat[:, cols]) * RANK_SCALE
-    finish(HALF - 3)
-    finish(HALF - 2)
-    steps(HALF + 3)
-    finish(HALF - 1)
-    finish(HALF)
+    steps(HALF + 4)
+    finish(5, 6)
+    finish(7)
+    steps(HALF + 5)
+    finish(8)
     for q in range(SIDE):
         cols = pl.ds(256 * q, 256)
         grad_buf[:SEQ_LEN, cols] = (acc[:SEQ_LEN, cols] * weight0).astype(BF16)
@@ -486,7 +494,7 @@
         send(
             src,
             recv_run.at[way, k, pl.ds(p * RS_PIECE, RS_PIECE), :],
-            rs_s.at[way, k, p],
+            rs_s,
             rs_r.at[way, k, p],
             dp,
             z_to(way),
@@ -504,11 +512,7 @@
         for p in range(RS_PIECES):
             rows = pl.ds(p * RS_PIECE, RS_PIECE)
             for way in live:
-                arrive(
-                    recv_run.at[way, k - 1, rows, :],
-                    rs_s.at[way, k - 1, p],
-                    rs_r.at[way, k - 1, p],
-                )
+                arrive(recv_run.at[way, k - 1, rows, :], rs_r.at[way, k - 1, p])
                 send_run[way, k, rows, :] = (
                     recv_run[way, k - 1, rows, :].astype(F32)
                     + own[rs_dest(way, k), rows, :].astype(F32)
@@ -519,7 +523,7 @@
         rows = pl.ds(p * RS_PIECE, RS_PIECE)
         for way in (0, 1):
             k = w_reach(way) - 1
-            arrive(recv_run.at[way, k, rows, :], rs_s.at[way, k, p], rs_r.at[way, k, p])
+            arrive(recv_run.at[way, k, rows, :], rs_r.at[way, k, p])
         stage[rows, :] = (
             recv_run[0, HALF - 1, rows, :].astype(F32)
             + recv_run[1, HALF - 2, rows, :].astype(F32)
@@ -530,17 +534,17 @@
     for g in range(GROUPS):
         send_back[g] = stage[pl.ds(g, 16, stride=GROUPS), :].astype(BF16)
 
-    @pl.loop(1, GROUPS)
-    def _(i):
-        to = lax.rem(dp + i, GROUPS)
-        remote(send_back.at[to], recv_back.at[dp], back_s.at[i], back_r.at[i], to, z).start()
+    exchange(send_back, recv_back, back_s, back_r)
+    all_sent(send_small.at[pl.ds(0, GROUPS - 1)], small_s)
+    all_sent(w_buf.at[0, 0, pl.ds(0, 15 * SLICE), :], wz_s)
+    all_sent(w_buf.at[0, 0, pl.ds(0, 45 * SLICE), :], p1_s)
+    all_sent(w_buf.at[:, 0, pl.ds(0, 45 * SLICE), :], p2_s)
+    all_sent(w_buf.at[:, 0, pl.ds(0, 60 * SLICE), :], die_s)
+    all_sent(ag_buf.at[pl.ds(0, 15)], ag_s)
+    all_sent(own.at[pl.ds(0, 15)], rs_s)
 
     recv_back[dp] = send_back[dp]
-
-    @pl.loop(1, GROUPS)
-    def _(i):
-        frm = wrap(dp - i, GROUPS)
-        arrive(recv_back.at[frm], back_s.at[i], back_r.at[i])
+    exchanged(recv_back, back_r)
 
     stage[...] = recv_back[...].astype(F32).reshape(GROUPS * 16, 128)
     for s in range(3):
@@ -551,18 +555,7 @@
             codes_sel, sums, (((0,), (0,)), ((), ())), preferred_element_type=F32
         )
 
-    for copy in sent:
-        copy.wait_send()
-
-    @pl.loop(1, GROUPS)
-    def _(i):
-        to = lax.rem(dp + i, GROUPS)
-        remote(
-            send_small.at[to], recv_small.at[dp], small_s.at[i], small_r.at[i], to, z
-        ).wait_send()
-        remote(
-            send_back.at[to], recv_back.at[dp], back_s.at[i], back_r.at[i], to, z
-        ).wait_send()
+    all_sent(send_back.at[pl.ds(0, GROUPS - 1)], back_s)
 
 
 def shards(
@@ -576,9 +569,11 @@
     return pl.pallas_call(
         step_kernel,
         out_shape=jax.ShapeDtypeStruct((128, 384), F32),
-        in_specs=[vmem, vmem, hbm, hbm, hbm, smem, vmem, vmem],
+        in_specs=[hbm, hbm, hbm, hbm, hbm, smem, vmem, vmem],
         out_specs=vmem,
         scratch_shapes=[
+            pltpu.VMEM((TASKS, 128), BF16),
+            pltpu.VMEM((128, 384), BF16),
             pltpu.VMEM((SIDE, 2, D, 128), BF16),
             pltpu.VMEM((TOK, D), BF16),
             pltpu.VMEM((TOK, KV), BF16),
@@ -599,22 +594,15 @@
             pltpu.VMEM((MEMBERS, ROWS, 128), BF16),
             pltpu.VMEM((2, HALF, ROWS, 128), BF16),
             pltpu.VMEM((2, HALF, ROWS, 128), BF16),
-            dma((10,)),
-            dma((GROUPS,)),
-            dma((GROUPS,)),
-            dma((GROUPS,)),
-            dma((GROUPS,)),
+            dma((5,)),
+            dma,
+            dma,
+            dma((8,)),
             dma((2, HALF)),
             dma((2, HALF)),
-            dma((2, HALF, 3)),
-            dma((2, HALF, 3)),
-            dma((2, HALF, 3)),
-            dma((2, HALF, 3)),
-            dma((2, HALF, 4)),
-            dma((2, HALF, 4)),
+            dma((2, HALF, 2)),
+            dma((2, HALF)),
             dma((2, HALF, PIECES)),
-            dma((2, HALF, PIECES)),
-            dma((2, HALF, RS_PIECES)),
             dma((2, HALF, RS_PIECES)),
         ],
         compiler_params=pltpu.CompilerParams(collective_id=0, has_side_effects=True),

time: 106 us -> 98.8 us (0.932)
  Pallas kernels: 104 us -> 97 us
    pallas_call x1, Pallas kernels: 104 us -> 97 us  [shards(): pl.pallas_call(step_kernel, out_shape=jax.ShapeDtypeStruct((128, 384), F3...]
where the time goes in v3:
time: 98.8 us; the launch traced here: 98.6 us
  Pallas kernels  97 us (98%)
  local copies, waits for them, and re-layouts  1.62 us (2%)
    pallas_call x1, Pallas kernels, shards(): pl.pallas_call(step_kernel, out_shape=jax.ShapeDtypeStruct((128, 384), F3...  97 us

profile of v3, /device:TPU:1, one launch (start us, length us, event | category | flops | bytes accessed | tf_op | source)
XLA Modules:
  0.0 98.6 jit_solution(15242302817230293588)
XLA Ops:
  0.0 97.0 %shard_map.82 = f32[128,384]{1,0:T(8,128)} custom-call(bf16[64,128]{1,0:T(8,128)(2,1)} %codes_hbm.1, bf16[128,384]{1,0:T(8,128)(2,1)} %hyper_hbm.1, bf16[320,1024]{1,0:T(8,128)(2,1)} %frozen_hbm.1, bf16[256,5120]{1,0:T(8,128)(2,1)} %tokens_hbm.1, bf16[256,1024]{1,0:T(8,128)(2,1)} %teacher_hbm.1, s32[2]{0:T(128)} %seq_ref.1, s32[1,32]{1,0:T(1,128)} %bitcast.2, ...), custom_call_target="tpu_custom_call" | custom-call | tf_op jit(solution)/shard_map/pallas_call | solution.py:569
  97.0 1.6 %copy.10 = f32[128,384]{1,0:T(8,128)} copy(f32[128,384]{1,0:T(8,128)} %shard_map.82) | data formatting | bytes 393216

commit v4 on v3

--- a/solution.py
+++ b/solution.py
@@ -131,26 +131,6 @@
     def all_sent(like, ssem):
         remote(like, like, ssem, small_r, dp, z).wait_send()
 
-    codes_copy = pltpu.make_async_copy(codes_hbm, codes_ref, local_sem.at[3])
-    hyper_copy = pltpu.make_async_copy(hyper_hbm, hyper_ref, local_sem.at[4])
-    codes_copy.start()
-    hyper_copy.start()
-
-    barrier = pltpu.get_barrier_semaphore()
-
-    def peer(offset, sign):
-        dy, dx, dc = offset
-        core = c if dc == 0 else 1 - c
-        return (wrap(y + sign * dy, SIDE) * SIDE + wrap(x + sign * dx, SIDE)) * 2 + core
-
-    for offset in PLANE:
-        pl.semaphore_signal(barrier, inc=1, device_id=(peer(offset, 1), z), device_id_type=MESH)
-
-    for shift in (1, -1):
-        pl.semaphore_signal(
-            barrier, inc=1, device_id=(dp, wrap(z + shift, MEMBERS)), device_id_type=MESH
-        )
-
     local = []
     for yy in range(SIDE):
         for cc in range(2):
@@ -161,12 +141,149 @@
                     local_sem.at[0],
                 )
             )
+    for copy in local:
+        copy.start()
+    codes_copy = pltpu.make_async_copy(codes_hbm, codes_ref, local_sem.at[3])
+    hyper_copy = pltpu.make_async_copy(hyper_hbm, hyper_ref, local_sem.at[4])
+    codes_copy.start()
+    hyper_copy.start()
+
     tok_copy = pltpu.make_async_copy(tokens_hbm, tok_buf, local_sem.at[1])
     teach_copy = pltpu.make_async_copy(teacher_hbm, teach_buf, local_sem.at[2])
-    for copy in local:
-        copy.start()
     tok_copy.start()
     teach_copy.start()
+
+    barrier = pltpu.get_barrier_semaphore()
+
+    def peer(offset, sign):
+        dy, dx, dc = offset
+        core = c if dc == 0 else 1 - c
+        return (wrap(y + sign * dy, SIDE) * SIDE + wrap(x + sign * dx, SIDE)) * 2 + core
+
+    for offset in PLANE:
+        pl.semaphore_signal(barrier, inc=1, device_id=(peer(offset, 1), z), device_id_type=MESH)
+
+    for shift in (1, -1, 2, -2):
+        pl.semaphore_signal(
+            barrier, inc=1, device_id=(dp, wrap(z + shift, MEMBERS)), device_id_type=MESH
+        )
+
+    pl.semaphore_wait(barrier, GROUPS + 3)
+
+    def w_block(way, d):
+        return wrap(z - f * d if way == 0 else z + f * d, MEMBERS)
+
+    def w_rows(start, size):
+        return pl.ds(pl.multiple_of(start, 16), size)
+
+    def w_slice(zb):
+        return w_buf.at[y, c, w_rows(BLK * zb + SLICE * x, SLICE), :]
+
+    def w_piece(way, phase, zb, i):
+        if way == 0 and phase == 1:
+            return w_buf.at[y, c, w_rows(BLK * zb + SLICE * i, SLICE), :]
+        if way == 0:
+            return w_buf.at[i, c, w_rows(BLK * zb, BLK), :]
+        if phase == 1:
+            return w_buf.at[i, c, w_rows(BLK * zb + SLICE * x, SLICE), :]
+        return w_buf.at[:, c, w_rows(BLK * zb + SLICE * i, SLICE), :]
+
+    def along(way, phase):
+        return x if (way == 0) == (phase == 1) else y
+
+    def shifted(way, phase, by):
+        if (way == 0) == (phase == 1):
+            return place(y, wrap(x + by, SIDE))
+        return place(wrap(y + by, SIDE), x)
+
+    def w_reach(way):
+        return HALF if way == 0 else HALF - 1
+
+    def z_to(way):
+        return wrap(z + f if way == 0 else z - f, MEMBERS)
+
+    def send_z(way, d):
+        ref = w_slice(w_block(way, d - 1))
+        send(ref, ref, wz_s, wz_r.at[way, d - 1], dp, z_to(way))
+
+    def plane_send(way, phase, d, frm, kind, by):
+        ref = w_piece(way, phase, w_block(way, d), wrap(along(way, phase) + frm, SIDE))
+        if phase == 1:
+            ssem, rsem = p1_s, p1_r.at[way, d - 1]
+        else:
+            ssem, rsem = p2_s, p2_r.at[way, d - 1, min(kind, 1)]
+        send(ref, ref, ssem, rsem, shifted(way, phase, by), z)
+
+    def twin_send(way, d, frm):
+        ref = w_piece(way, 2, w_block(way, d), wrap(along(way, 2) + frm, SIDE))
+        send(ref, ref, die_s, die_r.at[way, d - 1], dp + f, z)
+
+    def twin_block(way, d):
+        return wrap(z + f * d if way == 0 else z - f * d, MEMBERS)
+
+    def twin_wait(way, d):
+        arrive(
+            w_buf.at[:, 1 - c, w_rows(BLK * twin_block(way, d), BLK), :], die_r.at[way, d - 1]
+        )
+
+    def take_z(way, d):
+        ref = w_slice(w_block(way, d))
+        arrive(ref, wz_r.at[way, d - 1])
+        if d < w_reach(way):
+            send_z(way, d + 1)
+        plane_send(way, 1, d, 0, 0, f)
+        plane_send(way, 1, d, 0, 1, -f)
+        plane_send(way, 1, d, 0, 2, 2 * f)
+
+    def start_second(way, d):
+        arrive(w_buf.at[0, c, pl.ds(0, 3 * SLICE), :], p1_r.at[way, d - 1])
+        plane_send(way, 2, d, 0, 0, f)
+        plane_send(way, 2, d, 0, 1, -f)
+        twin_send(way, d, 0)
+
+    def relay_second(way, d):
+        arrive(
+            w_piece(way, 2, w_block(way, d), wrap(along(way, 2) - f, SIDE)), p2_r.at[way, d - 1, 0]
+        )
+        plane_send(way, 2, d, -f, 2, f)
+        twin_send(way, d, -f)
+
+    def end_second(way, d):
+        arrive(w_buf.at[0, c, pl.ds(0, 2 * BLK), :], p2_r.at[way, d - 1, 1])
+        twin_send(way, d, f)
+        twin_send(way, d, -2 * f)
+
+    def ag_piece(way, d, p):
+        return ag_buf.at[w_block(way, d), pl.ds(p * PIECE, PIECE), :]
+
+    def send_ag(way, d, p):
+        ref = ag_piece(way, d - 1, p)
+        send(ref, ref, ag_s, ag_r.at[way, d - 1, p], dp, z_to(way))
+
+    def get_ag(way, d, p):
+        arrive(ag_piece(way, d, p), ag_r.at[way, d - 1, p])
+        if d < w_reach(way):
+            send_ag(way, d + 1, p)
+
+    def spread(m):
+        block = jnp.concatenate(
+            [ag_buf[m, pl.ds(96 * slot, 96), :] for slot in range(TPG)], axis=1
+        )
+        moved = dot(block, perm_buf[...])
+        for s in range(3):
+            for j in range(4):
+                tall[pl.ds(12 * m + 4 * s + j, GROUPS, stride=192), :] = moved[
+                    32 * s : 32 * (s + 1), 128 * j : 128 * (j + 1)
+                ]
+        for slot in range(TPG):
+            for s in range(3):
+                last = ag_buf[m, pl.ds(96 * slot + 32 * s + 16, 16), :].astype(F32)
+                low_rows[slot, pl.ds(3 * m + s, 8, stride=48), :] = last[8:16]
+
+    own_rows = w_buf.at[:, :, w_rows(BLK * z, BLK), :]
+    pltpu.make_async_copy(own_rows, own_rows, local_sem.at[0]).wait()
+    for way in (0, 1):
+        send_z(way, 1)
 
     share = share_ref[...].astype(F32)
     g_row = lax.rem(iota((TPG * GROUPS, GROUPS), 0), GROUPS)
@@ -191,123 +308,6 @@
     for g in range(GROUPS):
         send_small[g] = stage[pl.ds(g, 16, stride=GROUPS), :].astype(BF16)
 
-    pl.semaphore_wait(barrier, GROUPS + 1)
-
-    def w_block(way, d):
-        return wrap(z - f * d if way == 0 else z + f * d, MEMBERS)
-
-    def w_rows(start, size):
-        return pl.ds(pl.multiple_of(start, 16), size)
-
-    def w_slice(zb):
-        return w_buf.at[y, c, w_rows(BLK * zb + SLICE * x, SLICE), :]
-
-    def w_piece(way, phase, zb, i):
-        if way == 0 and phase == 1:
-            return w_buf.at[y, c, w_rows(BLK * zb + SLICE * i, SLICE), :]
-        if way == 0:
-            return w_buf.at[i, c, w_rows(BLK * zb, BLK), :]
-        if phase == 1:
-            return w_buf.at[i, c, w_rows(BLK * zb + SLICE * x, SLICE), :]
-        return w_buf.at[:, c, w_rows(BLK * zb + SLICE * i, SLICE), :]
-
-    def along(way, phase):
-        return x if (way == 0) == (phase == 1) else y
-
-    def shifted(way, phase, by):
-        if (way == 0) == (phase == 1):
-            return place(y, wrap(x + by, SIDE))
-        return place(wrap(y + by, SIDE), x)
-
-    def w_reach(way):
-        return HALF if way == 0 else HALF - 1
-
-    def z_to(way):
-        return wrap(z + f if way == 0 else z - f, MEMBERS)
-
-    def send_z(way, d):
-        ref = w_slice(w_block(way, d - 1))
-        send(ref, ref, wz_s, wz_r.at[way, d - 1], dp, z_to(way))
-
-    def plane_send(way, phase, d, frm, kind, by):
-        ref = w_piece(way, phase, w_block(way, d), wrap(along(way, phase) + frm, SIDE))
-        if phase == 1:
-            ssem, rsem = p1_s, p1_r.at[way, d - 1]
-        else:
-            ssem, rsem = p2_s, p2_r.at[way, d - 1, min(kind, 1)]
-        send(ref, ref, ssem, rsem, shifted(way, phase, by), z)
-
-    def twin_send(way, d, frm):
-        ref = w_piece(way, 2, w_block(way, d), wrap(along(way, 2) + frm, SIDE))
-        send(ref, ref, die_s, die_r.at[way, d - 1], dp + f, z)
-
-    def twin_block(way, d):
-        return wrap(z + f * d if way == 0 else z - f * d, MEMBERS)
-
-    def twin_wait(way, d):
-        arrive(
-            w_buf.at[:, 1 - c, w_rows(BLK * twin_block(way, d), BLK), :], die_r.at[way, d - 1]
-        )
-
-    def take_z(way, d):
-        ref = w_slice(w_block(way, d))
-        arrive(ref, wz_r.at[way, d - 1])
-        if d < w_reach(way):
-            send_z(way, d + 1)
-        plane_send(way, 1, d, 0, 0, f)
-        plane_send(way, 1, d, 0, 1, -f)
-        plane_send(way, 1, d, 0, 2, 2 * f)
-
-    def start_second(way, d):
-        arrive(w_buf.at[0, c, pl.ds(0, 3 * SLICE), :], p1_r.at[way, d - 1])
-        plane_send(way, 2, d, 0, 0, f)
-        plane_send(way, 2, d, 0, 1, -f)
-        twin_send(way, d, 0)
-
-    def relay_second(way, d):
-        arrive(
-            w_piece(way, 2, w_block(way, d), wrap(along(way, 2) - f, SIDE)), p2_r.at[way, d - 1, 0]
-        )
-        plane_send(way, 2, d, -f, 2, f)
-        twin_send(way, d, -f)
-
-    def end_second(way, d):
-        arrive(w_buf.at[0, c, pl.ds(0, 2 * BLK), :], p2_r.at[way, d - 1, 1])
-        twin_send(way, d, f)
-        twin_send(way, d, -2 * f)
-
-    def ag_piece(way, d, p):
-        return ag_buf.at[w_block(way, d), pl.ds(p * PIECE, PIECE), :]
-
-    def send_ag(way, d, p):
-        ref = ag_piece(way, d - 1, p)
-        send(ref, ref, ag_s, ag_r.at[way, d - 1, p], dp, z_to(way))
-
-    def get_ag(way, d, p):
-        arrive(ag_piece(way, d, p), ag_r.at[way, d - 1, p])
-        if d < w_reach(way):
-            send_ag(way, d + 1, p)
-
-    def spread(m):
-        block = jnp.concatenate(
-            [ag_buf[m, pl.ds(96 * slot, 96), :] for slot in range(TPG)], axis=1
-        )
-        moved = dot(block, perm_buf[...])
-        for s in range(3):
-            for j in range(4):
-                tall[pl.ds(12 * m + 4 * s + j, GROUPS, stride=192), :] = moved[
-                    32 * s : 32 * (s + 1), 128 * j : 128 * (j + 1)
-                ]
-        for slot in range(TPG):
-            for s in range(3):
-                last = ag_buf[m, pl.ds(96 * slot + 32 * s + 16, 16), :].astype(F32)
-                low_rows[slot, pl.ds(3 * m + s, 8, stride=48), :] = last[8:16]
-
-    own_rows = w_buf.at[:, :, w_rows(BLK * z, BLK), :]
-    pltpu.make_async_copy(own_rows, own_rows, local_sem.at[0]).wait()
-    for way in (0, 1):
-        send_z(way, 1)
-
     def exchange(out, into, ssem, rsem):
         for offset in PLANE:
             to = peer(offset, 1)
@@ -327,17 +327,18 @@
     def at(d):
         return [w for w in ways if w[1] == d]
 
-    def frozen(blocks):
-        @pl.loop(0, SIDE)
-        def _(q):
-            cols = pl.ds(pl.multiple_of(256 * q, 256), 256)
+    def add_up(cols, total):
+        acc[:, cols] = acc[:, cols] + total
+
+    def frozen(blocks, put=add_up):
+        for q in range(SIDE):
             total = None
             for zb in blocks:
                 rows = w_rows(BLK * zb, BLK)
                 wide = jnp.concatenate([w_buf[q, 0, rows, :], w_buf[q, 1, rows, :]], axis=1)
                 part = dot(tok_blocks[zb], wide)
                 total = part if total is None else total + part
-            acc[:, cols] = acc[:, cols] + total
+            put(pl.ds(256 * q, 256), total)
 
     def prepare(k):
         for zb in (2 * k, 2 * k + 1):
@@ -350,8 +351,10 @@
         prepare(k)
     acc[...] = -teach_buf[...].astype(F32)
 
+    for way, d in at(1) + at(2):
+        take_z(way, d)
     for way, d in at(1):
-        take_z(way, d)
+        start_second(way, d)
 
     recv_small[dp] = send_small[dp]
 
@@ -366,27 +369,25 @@
             send_ag(way, 1, p)
     spread(z)
 
-    frozen([z])
-
     def get_piece(t, p):
-        for way, d in at(t - 1):
+        for way, d in at(t - 2):
             get_ag(way, d, p)
 
     def steps(t):
-        get_piece(t, 0)
         for way, d in at(t):
             take_z(way, d)
         for way, d in at(t - 1):
             start_second(way, d)
+        get_piece(t, 0)
         get_piece(t, 1)
+        for way, d in at(t - 4):
+            end_second(way, d)
+        get_piece(t, 2)
         for way, d in at(t - 3):
-            relay_second(way, d)
-        get_piece(t, 2)
-        for way, d in at(t - 5):
-            end_second(way, d)
-        for way, d in at(t - 2):
             spread(w_block(way, d))
         get_piece(t, 3)
+        for way, d in at(t - 2):
+            relay_second(way, d)
 
     def finish(*distances):
         blocks = [wd for d in distances for wd in at(d)]
@@ -394,14 +395,14 @@
             twin_wait(way, d)
         frozen([w_block(way, d) for way, d in blocks])
 
-    for t in range(2, HALF + 3):
+    steps(3)
+    frozen([z])
+    for t in range(4, HALF + 4):
         steps(t)
-        if t == 8:
+        if t == 7:
             finish(1, 2)
-        if t == 10:
+        if t == 9:
             finish(3, 4)
-
-    steps(HALF + 3)
 
     seq0 = seq_ref[0]
     seq1 = seq_ref[1]
@@ -436,15 +437,18 @@
     for q in range(SIDE):
         cols = pl.ds(256 * q, 256)
         acc[:, cols] = acc[:, cols] + dot(low, b_mat[:, cols]) * RANK_SCALE
+    finish(5, 6)
     steps(HALF + 4)
-    finish(5, 6)
     finish(7)
-    steps(HALF + 5)
-    finish(8)
-    for q in range(SIDE):
-        cols = pl.ds(256 * q, 256)
-        grad_buf[:SEQ_LEN, cols] = (acc[:SEQ_LEN, cols] * weight0).astype(BF16)
-        grad_buf[SEQ_LEN:, cols] = (acc[SEQ_LEN:, cols] * weight1).astype(BF16)
+
+    def weigh(cols, total):
+        full = acc[:, cols] + total
+        grad_buf[:SEQ_LEN, cols] = (full[:SEQ_LEN] * weight0).astype(BF16)
+        grad_buf[SEQ_LEN:, cols] = (full[SEQ_LEN:] * weight1).astype(BF16)
+
+    for way, d in at(HALF):
+        twin_wait(way, d)
+    frozen([w_block(way, d) for way, d in at(HALF)], weigh)
 
     grad = grad_buf[...]
     low_grad = lax.dot_general(
@@ -491,21 +495,23 @@
         return wrap(z + f * (HALF - k) if way == 0 else z - f * (HALF - 1 - k), MEMBERS)
 
     def run_send(way, k, p, src):
+        far = wrap(z + 2 * f if way == 0 else z - 2 * f, MEMBERS)
         send(
             src,
             recv_run.at[way, k, pl.ds(p * RS_PIECE, RS_PIECE), :],
             rs_s,
             rs_r.at[way, k, p],
             dp,
-            z_to(way),
-        )
-
-    for way in (0, 1):
-        m = rs_dest(way, 0)
-        collect(m)
-        for p in range(RS_PIECES):
-            run_send(way, 0, p, own.at[m, pl.ds(p * RS_PIECE, RS_PIECE), :])
-    for k in range(1, HALF):
+            far if k == 0 else z_to(way),
+        )
+
+    for k in (0, 1):
+        for way in (0, 1):
+            m = rs_dest(way, k)
+            collect(m)
+            for p in range(RS_PIECES):
+                run_send(way, k, p, own.at[m, pl.ds(p * RS_PIECE, RS_PIECE), :])
+    for k in range(2, HALF):
         live = [way for way in (0, 1) if k < w_reach(way)]
         for way in live:
             collect(rs_dest(way, k))
@@ -513,10 +519,13 @@
             rows = pl.ds(p * RS_PIECE, RS_PIECE)
             for way in live:
                 arrive(recv_run.at[way, k - 1, rows, :], rs_r.at[way, k - 1, p])
-                send_run[way, k, rows, :] = (
-                    recv_run[way, k - 1, rows, :].astype(F32)
-                    + own[rs_dest(way, k), rows, :].astype(F32)
-                ).astype(BF16)
+                total = recv_run[way, k - 1, rows, :].astype(F32) + own[
+                    rs_dest(way, k), rows, :
+                ].astype(F32)
+                if k == 2:
+                    arrive(recv_run.at[way, 0, rows, :], rs_r.at[way, 0, p])
+                    total = total + recv_run[way, 0, rows, :].astype(F32)
+                send_run[way, k, rows, :] = total.astype(BF16)
                 run_send(way, k, p, send_run.at[way, k, rows, :])
     collect(z)
     for p in range(RS_PIECES):

time: 98.8 us -> 96.6 us (0.978)
  Pallas kernels: 97 us -> 94.8 us
    pallas_call x1, Pallas kernels: 97 us -> 94.8 us  [shards(): pl.pallas_call(step_kernel, out_shape=jax.ShapeDtypeStruct((128, 384), F3...]
where the time goes in v4:
time: 96.6 us; the launch traced here: 96.4 us
  Pallas kernels  94.8 us (98%)
  local copies, waits for them, and re-layouts  1.62 us (2%)
    pallas_call x1, Pallas kernels, shards(): pl.pallas_call(step_kernel, out_shape=jax.ShapeDtypeStruct((128, 384), F3...  94.8 us

profile of v4, /device:TPU:1, one launch (start us, length us, event | category | flops | bytes accessed | tf_op | source)
XLA Modules:
  0.0 96.4 jit_solution(3251075559165983925)
XLA Ops:
  0.0 94.8 %shard_map.82 = f32[128,384]{1,0:T(8,128)} custom-call(bf16[64,128]{1,0:T(8,128)(2,1)} %codes_hbm.1, bf16[128,384]{1,0:T(8,128)(2,1)} %hyper_hbm.1, bf16[320,1024]{1,0:T(8,128)(2,1)} %frozen_hbm.1, bf16[256,5120]{1,0:T(8,128)(2,1)} %tokens_hbm.1, bf16[256,1024]{1,0:T(8,128)(2,1)} %teacher_hbm.1, s32[2]{0:T(128)} %seq_ref.1, s32[1,32]{1,0:T(1,128)} %bitcast.2, ...), custom_call_target="tpu_custom_call" | custom-call | tf_op jit(solution)/shard_map/pallas_call | solution.py:578
  94.8 1.6 %copy.10 = f32[128,384]{1,0:T(8,128)} copy(f32[128,384]{1,0:T(8,128)} %shard_map.82) | data formatting | bytes 393216

commit v5 on v4

--- a/solution.py
+++ b/solution.py
@@ -345,13 +345,16 @@
             tok_blocks[zb] = tok_buf[:, BLK * zb : BLK * (zb + 1)]
         tok_t[pl.ds(2 * BLK * k, 2 * BLK), :] = tok_buf[:, 2 * BLK * k : 2 * BLK * (k + 1)].T
 
+    for way, d in at(1):
+        take_z(way, d)
+
     tok_copy.wait()
     teach_copy.wait()
     for k in range(MEMBERS // 2):
         prepare(k)
     acc[...] = -teach_buf[...].astype(F32)
 
-    for way, d in at(1) + at(2):
+    for way, d in at(2):
         take_z(way, d)
     for way, d in at(1):
         start_second(way, d)

time: 96.6 us -> 96.2 us (level)
  no operation moved by 1% of the time
where the time goes in v5:
time: 96.2 us; the launch traced here: 96 us
  Pallas kernels  94.4 us (98%)
  local copies, waits for them, and re-layouts  1.62 us (2%)
    pallas_call x1, Pallas kernels, shards(): pl.pallas_call(step_kernel, out_shape=jax.ShapeDtypeStruct((128, 384), F3...  94.4 us

profile of v5, /device:TPU:1, one launch (start us, length us, event | category | flops | bytes accessed | tf_op | source)
XLA Modules:
  0.0 96.0 jit_solution(14664457328109094029)
XLA Ops:
  0.0 94.4 %shard_map.82 = f32[128,384]{1,0:T(8,128)} custom-call(bf16[64,128]{1,0:T(8,128)(2,1)} %codes_hbm.1, bf16[128,384]{1,0:T(8,128)(2,1)} %hyper_hbm.1, bf16[320,1024]{1,0:T(8,128)(2,1)} %frozen_hbm.1, bf16[256,5120]{1,0:T(8,128)(2,1)} %tokens_hbm.1, bf16[256,1024]{1,0:T(8,128)(2,1)} %teacher_hbm.1, s32[2]{0:T(128)} %seq_ref.1, s32[1,32]{1,0:T(1,128)} %bitcast.2, ...), custom_call_target="tpu_custom_call" | custom-call | tf_op jit(solution)/shard_map/pallas_call | solution.py:581
  94.4 1.6 %copy.10 = f32[128,384]{1,0:T(8,128)} copy(f32[128,384]{1,0:T(8,128)} %shard_map.82) | data formatting | bytes 393216
